TPU v7x, 256 devices: a whole 4x4x8 slice. The times are simulated.
256 devices in a mesh: dp: 4 (over y_lo, core), tm: 4 (over x), rows: 16 (over z, y_hi).
Axes of the slice: x: 4, y: 4 (y_hi: 2, y_lo: 2; y = y_hi * 2 + y_lo), z: 8, core: 2. Of those that a mesh axis runs over, the one named last changes fastest.
Arguments:
- latents: bfloat16 [4, 8, 16, 30, 512], P('dp', 'tm', 'rows'), may hold values from -6 to 6
- grad_out: bfloat16 [4, 8, 32, 60, 256], P('dp', 'tm', 'rows'), may hold values from -6 to 6
- kernel: bfloat16 [3, 3, 3, 512, 256], replicated, may hold values from -0.0546875 to 0.0546875
Outputs:
- grad_latents: bfloat16 [4, 8, 16, 30, 512], P('dp', 'tm', 'rows')
- weight_grad: float32 [512, 3, 3, 3, 256], P(('dp', 'tm', 'rows'))
All inputs are finite; a program needn't handle non-finite values.
Results may differ from a plain program's by a relative error of at most 0.001.
Values may be sent and summed in bfloat16 or wider, within the bound.
A program may use at most 128 MiB of HBM per device.

v0:
```python
import jax
import jax.numpy as jnp
from jax import lax
from jax.sharding import PartitionSpec as P


def shift_from(shard, axis, by):
    peers = lax.axis_size(axis)
    pairs = [(i, i + by) for i in range(peers) if 0 <= i + by < peers]
    return lax.ppermute(shard, axis, pairs)


def pool_pairs(values, dim):
    n = values.shape[dim] // 2
    pad = [(0, 0)] * values.ndim
    pad[dim] = (1, 1)
    ext = jnp.pad(values, pad)
    out = []
    for i in range(3):
        start = 2 - i
        a = lax.slice_in_dim(ext, start, start + 2 * n - 1, stride=2, axis=dim)
        b = lax.slice_in_dim(ext, start + 1, start + 2 * n, stride=2, axis=dim)
        out.append(a + b)
    return jnp.stack(out, axis=dim + 1)


def body(latents, grad_out, kernel):
    frames = grad_out.shape[1]
    height = grad_out.shape[2]
    width = grad_out.shape[3]
    channels = latents.shape[4]
    outputs = grad_out.shape[4]
    devices = lax.axis_size("dp") * lax.axis_size("tm") * lax.axis_size("rows")
    factor = float(devices * frames * height * width) ** (-0.5)
    slab_count = lax.axis_size("rows")
    slab = lax.axis_index("rows")

    grad_whole = lax.all_gather(grad_out[0], "rows", axis=1, tiled=True)
    whole_height = grad_whole.shape[1]

    padded_rows = jnp.pad(grad_whole, ((0, 0), (1, 1), (0, 0), (0, 0)))
    near = lax.dynamic_slice_in_dim(padded_rows, slab * height, height + 2, axis=1)
    later = shift_from(near, "tm", -1)
    grad_all = jnp.concatenate([near, later], axis=0)
    grad_all = jnp.pad(grad_all, ((0, 0), (0, 0), (1, 1), (0, 0)))
    patches = []
    for a in range(3):
        for i in range(3):
            for j in range(3):
                patches.append(
                    grad_all[2 - a : 2 - a + frames, 2 - i : 2 - i + height, 2 - j : 2 - j + width]
                )
    patches = jnp.stack(patches, axis=3).reshape(frames * height * width, 27, outputs)
    grad_up = lax.dot_general(
        patches,
        kernel.reshape(27, channels, outputs),
        (((1, 2), (0, 2)), ((), ())),
        preferred_element_type=jnp.float32,
    )
    pooled = grad_up.reshape(frames, height // 2, 2, width // 2, 2, channels).sum(axis=(2, 4))
    grad_latents = pooled.astype(jnp.bfloat16)[None]

    groups = lax.axis_size("dp") * lax.axis_size("tm")
    share = channels // devices
    earlier = shift_from(latents, "tm", 1)
    with_earlier = jnp.concatenate([earlier, latents], axis=1)
    lead = with_earlier.shape[:4]
    regrouped = with_earlier.reshape(lead + (groups, slab_count, share))
    regrouped = jnp.swapaxes(regrouped, 4, 5).reshape(lead + (channels,))
    owned = lax.all_to_all(regrouped, "rows", split_axis=4, concat_axis=2, tiled=True)[0]
    group_channels = owned.shape[3]
    taps_a = jnp.stack([owned[a : a + frames] for a in range(3)], axis=0)

    pooled_grad = pool_pairs(pool_pairs(grad_whole.astype(jnp.float32), 1), 3)
    scaled = pooled_grad * 65537.0
    top = scaled - (scaled - pooled_grad)
    both = jnp.stack([top, pooled_grad - top], axis=0).astype(jnp.bfloat16)
    term = jnp.einsum(
        "afrsc,xfrisjo->caijxo", taps_a, both, preferred_element_type=jnp.float32
    )
    term = (term[..., 0, :] + term[..., 1, :]) * factor
    term = term.reshape(group_channels, 3, 3, 3, outputs)
    term = lax.psum_scatter(term, "dp", scatter_dimension=0, tiled=True)
    weight_grad = lax.psum_scatter(term, "tm", scatter_dimension=0, tiled=True)
    return (grad_latents, weight_grad)


def solution(mesh):
    in_specs = (P("dp", "tm", "rows", None, None), P("dp", "tm", "rows", None, None), P())
    out_specs = (P("dp", "tm", "rows", None, None), P(("dp", "tm", "rows"), None, None, None, None))
    return jax.shard_map(body, mesh=mesh, in_specs=in_specs, out_specs=out_specs, check_vma=False)
```

profile of v0, /device:TPU:1, one launch (start us, length us, event | category | flops | bytes accessed | tf_op | source)
XLA Modules:
  0.0 253.7 jit_solution(13434810595302571663)
XLA Ops:
  7.2 1.6 copy.131
  8.8 4.0 %collective-permute-start.1 = (bf16[1,2,1,30,512]{4,1,3,2,0:T(2,128)(2,1)}, bf16[1,2,1,30,512]{4,1,3,2,0:T(2,128)(2,1)S(1)}, u32[]{:S(2)}, u32[]{:S(2)}) collective-permute-start(bf16[1,2,1,30,512]{4,1,3,2,0:T(2,128)(2,1)} %param.3), channel_id=1, source_target_pairs={{0,16},{16,32},{32,48},{1,17},{17,33},{33,49},{2,18},{18,34},{34,5... | collective-permute-start | bytes 184328 | tf_op jit(solution)/shard_map/ppermute | solution.py:10
  12.8 1.6 collective-permute-done.1
  14.4 1.0 pad_maximum_fusion.2
  15.3 0.3 copy.188
  15.6 0.4 copy.189
  16.0 0.4 copy.229
  16.4 1.6 reshape.331
  18.1 10.9 %all-to-all-start = ((bf16[16,2,1920]{2,1,0:T(2,128)(2,1)}), bf16[16,2,1920]{2,1,0:T(2,128)(2,1)S(1)}, u32[]{:S(2)}, u32[]{:S(2)}) async-start(bf16[16,2,1920]{2,1,0:T(2,128)(2,1)} %reshape.331), calls=%async_computation | async-start | bytes 245760 | tf_op jit(solution)/shard_map/all_to_all | solution.py:70
  29.1 0.6 dynamic-slice
  30.3 9.3 %all-to-all-done = bf16[16,2,1920]{2,1,0:T(2,128)(2,1)S(1)} async-done(((bf16[16,2,1920]{2,1,0:T(2,128)(2,1)}), bf16[16,2,1920]{2,1,0:T(2,128)(2,1)S(1)}, u32[]{:S(2)}, u32[]{:S(2)}) %all-to-all-start) | async-done | bytes 122912 | tf_op jit(solution)/shard_map/all_to_all | solution.py:70
  39.6 1.4 reshape.332
  41.2 55.2 %all-gather.3.cloned.1.call-done = bf16[1,2,32,60,256]{4,3,2,1,0:T(8,128)(2,1)} async-done(((bf16[1,2,2,60,256]{4,3,2,1,0:T(8,128)(2,1)}), bf16[1,2,32,60,256]{4,3,2,1,0:T(8,128)(2,1)}) %all-gather.3.cloned.1.call-update) | async-done | bytes 1966096 | tf_op jit(solution)/shard_map/all_gather | solution.py:38
  96.4 1.1 pad_dynamic-slice_fusion.3
  97.5 0.6 copy-done
  98.1 0.6 pad_convert_fusion
  98.7 1.0 add_bitcast_fusion.5
  99.7 3.3 %select_maximum_fusion = f32[2,16,3,62,256]{4,3,1,0,2:T(8,128)} fusion(f32[2,16,1,60,256]{4,3,1,0,2:T(8,128)S(1)} %get-tuple-element.14, f32[2,16,1,60,256]{4,3,1,0,2:T(8,128)S(1)} %get-tuple-element.13, f32[2,16,1,60,256]{4,3,1,0,2:T(8,128)S(1)} %get-tuple-element.12), kind=kLoop, calls=%fused_computation.11 | loop fusion | flops 12189696 | bytes 11993088 | tf_op jit(solution)/shard_map/stack | solution.py:24
  103.0 14.3 %slice.173 = f32[2,16,3,30,256]{4,3,1,0,2:T(8,128)} slice(f32[2,16,3,62,256]{4,3,1,0,2:T(8,128)} %select_maximum_fusion), slice={[0:2:1], [0:16:1], [0:3:1], [2:61:2], [0:256:1]} | slice | bytes 5898240 | tf_op jit(solution)/shard_map/slice | solution.py:21
  117.3 14.3 %slice.174 = f32[2,16,3,30,256]{4,3,1,0,2:T(8,128)} slice(f32[2,16,3,62,256]{4,3,1,0,2:T(8,128)} %select_maximum_fusion), slice={[0:2:1], [0:16:1], [0:3:1], [3:62:2], [0:256:1]} | slice | bytes 5898240 | tf_op jit(solution)/shard_map/slice | solution.py:22
  131.6 14.2 %slice.175 = f32[2,16,3,30,256]{4,3,1,0,2:T(8,128)} slice(f32[2,16,3,62,256]{4,3,1,0,2:T(8,128)} %select_maximum_fusion), slice={[0:2:1], [0:16:1], [0:3:1], [1:60:2], [0:256:1]} | slice | bytes 5898240 | tf_op jit(solution)/shard_map/slice | solution.py:21
  145.8 14.2 %slice.176 = f32[2,16,3,30,256]{4,3,1,0,2:T(8,128)} slice(f32[2,16,3,62,256]{4,3,1,0,2:T(8,128)} %select_maximum_fusion), slice={[0:2:1], [0:16:1], [0:3:1], [0:59:2], [0:256:1]} | slice | bytes 5898240 | tf_op jit(solution)/shard_map/slice | solution.py:21
  160.0 1.3 collective-permute-start
  161.8 7.2 %add_bitcast_fusion.2 = (f32[1,2,16,3,30,1,256]{6,4,2,1,5,3,0:T(8,128)S(1)}, f32[1,2,16,3,30,1,256]{6,4,2,1,5,3,0:T(8,128)S(1)}, f32[1,2,16,3,30,1,256]{6,4,2,1,5,3,0:T(8,128)S(1)}) fusion(f32[2,16,3,30,256]{4,3,1,0,2:T(8,128)} %slice.173, f32[2,16,3,30,256]{4,3,1,0,2:T(8,128)} %slice.174, f32[2,16,3,30,256]{4,3,1,0,2:T(8,128)} %slice.175, ...), kind=kLoop, calls=%fused_computation.18 | loop fusion | flops 2211840 | bytes 20643840 | tf_op jit(solution)/shard_map/stack | solution.py:24
  169.0 2.2 fusion.1
  171.3 1.7 fusion.9
  173.0 1.1 fusion.17
  174.1 0.2 all-reduce.7.cloned.1.call-start
  174.4 0.2 pad_slice_fusion.7
  174.6 0.2 pad_slice_fusion.6
  174.9 0.1 copy.132
  175.0 0.7 copy_dynamic-update-slice_fusion.26
  178.9 0.7 copy_dynamic-update-slice_fusion.25
  179.6 0.7 copy_dynamic-update-slice_fusion.24
  180.3 0.7 copy_dynamic-update-slice_fusion.23
  180.9 0.7 copy_dynamic-update-slice_fusion.22
  181.6 0.7 copy_dynamic-update-slice_fusion.21
  182.3 0.7 copy_dynamic-update-slice_fusion.20
  183.0 0.7 copy_dynamic-update-slice_fusion.19
  183.6 0.7 copy_dynamic-update-slice_fusion.18
  184.3 0.7 copy_dynamic-update-slice_fusion.17
  185.0 0.7 copy_dynamic-update-slice_fusion.16
  185.7 0.7 copy_dynamic-update-slice_fusion.15
  186.3 0.7 copy_dynamic-update-slice_fusion.14
  187.0 0.7 copy_dynamic-update-slice_fusion.13
  187.6 0.7 copy_dynamic-update-slice_fusion.12
  188.3 0.7 copy_dynamic-update-slice_fusion.11
  189.0 0.7 copy_dynamic-update-slice_fusion.10
  189.7 0.7 copy_dynamic-update-slice_fusion.9
  190.4 0.7 copy_dynamic-update-slice_fusion.8
  191.0 0.7 copy_dynamic-update-slice_fusion.7
  191.7 0.7 copy_dynamic-update-slice_fusion.6
  192.4 0.7 copy_dynamic-update-slice_fusion.5
  193.1 0.7 copy_dynamic-update-slice_fusion.4
  193.7 0.7 copy_dynamic-update-slice_fusion.3
  194.4 0.7 copy_dynamic-update-slice_fusion.2
  195.1 0.7 copy_dynamic-update-slice_fusion.1
  195.8 0.7 copy_dynamic-update-slice_fusion
  196.4 1.8 reduce-scatter.3.cloned.1.call-done
  198.3 6.1 %fusion.13 = bf16[2,30,512]{2,1,0:T(8,128)(2,1)S(1)} fusion(bf16[27,512,256,1,1,1]{2,1,0,5,4,3:T(8,128)(2,1)} %bitcast.141, bf16[2,1,2,30,2,27,256]{6,3,5,4,2,0,1:T(8,128)(2,1)} %copy_dynamic-update-slice_fusion), kind=kOutput, calls=%fused_computation.29 | convolution fusion | flops 1698785280 | bytes 10457088 | tf_op jit(solution)/shard_map/dot_general | solution.py:54
  204.4 0.7 copy.192
  205.1 40.5 %all-reduce.7.cloned.1.call-done = f32[8,3,3,3,256]{4,0,1,3,2:T(8,128)} async-done(((f32[8,3,3,3,256]{4,0,1,3,2:T(8,128)}), f32[8,3,3,3,256]{4,0,1,3,2:T(8,128)}) %all-reduce.7.cloned.1.call-update) | async-done | bytes 221200
  245.6 1.0 constant_dynamic-slice_fusion
  246.5 0.6 copy.193
  (40 shorter events, 3.9 us)
Async XLA Ops:
  7.2 21.9 %copy-start.1 = (u32[256]{0:T(256)S(1)}, u32[256]{0:T(256)}, u32[]{:S(2)}) copy-start(u32[256]{0:T(256)} %constant.32) | copy-start | bytes 3076
  7.2 89.2 %all-gather.3.cloned.1.call-start = ((), (), s32[]{:S(2)}) async-start(), calls=%async_computation.3 | async-start | bytes 2228224 | tf_op jit(solution)/shard_map/all_gather | solution.py:38
  8.8 5.5 %collective-permute-start.1 = (bf16[1,2,1,30,512]{4,1,3,2,0:T(2,128)(2,1)}, bf16[1,2,1,30,512]{4,1,3,2,0:T(2,128)(2,1)S(1)}, u32[]{:S(2)}, u32[]{:S(2)}) collective-permute-start(bf16[1,2,1,30,512]{4,1,3,2,0:T(2,128)(2,1)} %param.3), channel_id=1, source_target_pairs={{0,16},{16,32},{32,48},{1,17},{17,33},{33,49},{2,18},{18,34},{34,5... | collective-permute-start | bytes 184328 | tf_op jit(solution)/shard_map/ppermute | solution.py:10
  18.1 21.5 %all-to-all-start = ((bf16[16,2,1920]{2,1,0:T(2,128)(2,1)}), bf16[16,2,1920]{2,1,0:T(2,128)(2,1)S(1)}, u32[]{:S(2)}, u32[]{:S(2)}) async-start(bf16[16,2,1920]{2,1,0:T(2,128)(2,1)} %reshape.331), calls=%async_computation | async-start | bytes 245760 | tf_op jit(solution)/shard_map/all_to_all | solution.py:70
  29.0 169.2 %reduce-scatter.3.cloned.1.call-start = ((), (), s32[]{:S(2)}) async-start(), calls=%async_computation.2 | async-start | bytes 1105920 | tf_op jit(solution)/shard_map/reduce_scatter | solution.py:83
  96.4 1.7 copy-start
  160.0 14.3 %collective-permute-start = (bf16[2,4,60,256]{3,2,1,0:T(8,128)(2,1)S(1)}, bf16[2,4,60,256]{3,2,1,0:T(8,128)(2,1)S(1)}, u32[]{:S(2)}, u32[]{:S(2)}) collective-permute-start(bf16[2,4,60,256]{3,2,1,0:T(8,128)(2,1)S(1)} %pad_dynamic-slice_fusion.3), channel_id=1, source_target_pairs={{16,0},{32,16},{48,32},{17,1},{33,17},{49,33},{18,2},{34,18},{50,3... | collective-permute-start | bytes 737288 | tf_op jit(solution)/shard_map/ppermute | solution.py:10
  174.1 71.5 %all-reduce.7.cloned.1.call-start = ((), (), s32[]{:S(2)}) async-start(), calls=%async_computation.4 | async-start | bytes 442368
Sparse Core Ops, SparseCore 0:
  10.6 85.7 all-gather.2
  174.2 23.9 reduce-scatter.2
  200.6 44.9 all-reduce.6
where the time goes:
time: 257 us; the launch traced here: 254 us
  waiting for transfers between devices  108 us (42%)
  local copies, waits for them, and re-layouts  89.7 us (35%)
  starting transfers between devices  16.5 us (6%)
  other arithmetic  16.5 us (6%)
  between operations  14.8 us (6%)
  matrix products  7.84 us (3%)
    all_gather x1, waiting for transfers between devices, body(): grad_whole = lax.all_gather(grad_out[0], 'rows', axis=1, tiled=True)  55.2 us
    slice x3, local copies, waits for them, and re-layouts, pool_pairs(): a = lax.slice_in_dim(ext, start, start + 2 * n - 1, stride=2, axis=dim)  42.7 us
    unnamed x4, waiting for transfers between devices  40.6 us
    unnamed x37, local copies, waits for them, and re-layouts  25.6 us
    slice x1, local copies, waits for them, and re-layouts, pool_pairs(): b = lax.slice_in_dim(ext, start + 1, start + 2 * n, stride=2, axis=dim)  14.3 us
    another operation x3, other arithmetic, pool_pairs(): return jnp.stack(out, axis=dim + 1)  11.5 us
    all_to_all x1, starting transfers between devices, body(): lax.all_to_all(regrouped, 'rows', split_axis=4, concat_axis=2, tiled=True)  10.9 us
    all_to_all x1, waiting for transfers between devices, body(): lax.all_to_all(regrouped, 'rows', split_axis=4, concat_axis=2, tiled=True)  9.3 us
  transfers between devices with their start and end apart: 6, of which 5 were waited for; matrix products, arithmetic and copies ran while one was open for 19% of the time, Pallas kernels for 0%

commit v1 on v0

--- a/solution.py
+++ b/solution.py
@@ -15,13 +15,26 @@
     pad = [(0, 0)] * values.ndim
     pad[dim] = (1, 1)
     ext = jnp.pad(values, pad)
-    out = []
-    for i in range(3):
-        start = 2 - i
-        a = lax.slice_in_dim(ext, start, start + 2 * n - 1, stride=2, axis=dim)
-        b = lax.slice_in_dim(ext, start + 1, start + 2 * n, stride=2, axis=dim)
-        out.append(a + b)
+    shape = values.shape
+    shifted = ext.reshape(shape[:dim] + (n + 1, 2) + shape[dim + 1 :]).sum(axis=dim + 1)
+    aligned = values.reshape(shape[:dim] + (n, 2) + shape[dim + 1 :]).sum(axis=dim + 1)
+    out = [
+        lax.slice_in_dim(shifted, 1, n + 1, axis=dim),
+        aligned,
+        lax.slice_in_dim(shifted, 0, n, axis=dim),
+    ]
     return jnp.stack(out, axis=dim + 1)
+
+
+def with_halo(block, axis, dim, width):
+    count = lax.axis_size(axis)
+    forward = [(i, i + 1) for i in range(count - 1)]
+    backward = [(target, source) for source, target in forward]
+    low = lax.ppermute(
+        lax.slice_in_dim(block, block.shape[dim] - width, None, axis=dim), axis, forward
+    )
+    high = lax.ppermute(lax.slice_in_dim(block, 0, width, axis=dim), axis, backward)
+    return jnp.concatenate([low, block, high], axis=dim)
 
 
 def body(latents, grad_out, kernel):
@@ -33,13 +46,11 @@
     devices = lax.axis_size("dp") * lax.axis_size("tm") * lax.axis_size("rows")
     factor = float(devices * frames * height * width) ** (-0.5)
     slab_count = lax.axis_size("rows")
-    slab = lax.axis_index("rows")
 
     grad_whole = lax.all_gather(grad_out[0], "rows", axis=1, tiled=True)
     whole_height = grad_whole.shape[1]
 
-    padded_rows = jnp.pad(grad_whole, ((0, 0), (1, 1), (0, 0), (0, 0)))
-    near = lax.dynamic_slice_in_dim(padded_rows, slab * height, height + 2, axis=1)
+    near = with_halo(grad_out[0], "rows", 1, 1)
     later = shift_from(near, "tm", -1)
     grad_all = jnp.concatenate([near, later], axis=0)
     grad_all = jnp.pad(grad_all, ((0, 0), (0, 0), (1, 1), (0, 0)))

time: 257 us -> 251 us (0.977)
  local copies, waits for them, and re-layouts: 89.7 us -> 61.5 us
  other arithmetic: 16.5 us -> 32.8 us
  starting transfers between devices: 16.5 us -> 23.4 us
    slice x4 -> x5, local copies, waits for them, and re-layouts: 57 us -> 20.3 us  [the longest x3 18.5 us: pool_pairs(): lax.slice_in_dim(shifted, 1, n + 1, axis=dim)]
    reduce_scatter x1, waiting for transfers between devices: 1.79 us -> 17.3 us  [body(): term = lax.psum_scatter(term, 'dp', scatter_dimension=0, tiled=True)]
    all_gather x1, waiting for transfers between devices: 55.2 us -> 40 us  [body(): grad_whole = lax.all_gather(grad_out[0], 'rows', axis=1, tiled=True)]
    reduce_sum x0 -> x3, other arithmetic: none -> 10.9 us  [the longest x2 5.59 us: pool_pairs(): values.reshape(shape[:dim] + (n, 2) + shape[dim + 1:]).sum(axis=dim + 1)]
    unnamed x0 -> x1, other arithmetic: none -> 7.74 us
    ppermute x0 -> x2, starting transfers between devices: none -> 6.12 us  [the longest x1 4.83 us: with_halo(): lax.ppermute(lax.slice_in_dim(block, block.shape[dim] - width, None, axis...]
    another operation x3 -> x1, other arithmetic: 11.5 us -> 5.48 us  [pool_pairs(): return jnp.stack(out, axis=dim + 1)]
    reduce_sum x0 -> x2, local copies, waits for them, and re-layouts: none -> 3.56 us  [pool_pairs(): values.reshape(shape[:dim] + (n, 2) + shape[dim + 1:]).sum(axis=dim + 1)]
  transfers between devices with their start and end apart: 6 -> 8, of which waited for: 5 -> 4; matrix products, arithmetic and copies ran while one was open for 19% -> 16% of each run, Pallas kernels for 0% -> 0%
where the time goes in v1:
time: 251 us; the launch traced here: 246 us
  waiting for transfers between devices  106 us (42%)
  local copies, waits for them, and re-layouts  61.5 us (25%)
  other arithmetic  32.8 us (13%)
  starting transfers between devices  23.4 us (9%)
  between operations  15 us (6%)
  matrix products  7.87 us (3%)
    unnamed x4, waiting for transfers between devices  40.6 us
    all_gather x1, waiting for transfers between devices, body(): grad_whole = lax.all_gather(grad_out[0], 'rows', axis=1, tiled=True)  40 us
    unnamed x59, local copies, waits for them, and re-layouts  27.8 us
    slice x3, local copies, waits for them, and re-layouts, pool_pairs(): lax.slice_in_dim(shifted, 1, n + 1, axis=dim)  18.5 us
    reduce_scatter x1, waiting for transfers between devices, body(): term = lax.psum_scatter(term, 'dp', scatter_dimension=0, tiled=True)  17.3 us
    all_to_all x1, starting transfers between devices, body(): lax.all_to_all(regrouped, 'rows', split_axis=4, concat_axis=2, tiled=True)  11.6 us
    all_to_all x1, waiting for transfers between devices, body(): lax.all_to_all(regrouped, 'rows', split_axis=4, concat_axis=2, tiled=True)  7.82 us
    unnamed x1, other arithmetic  7.74 us
  transfers between devices with their start and end apart: 8, of which 4 were waited for; matrix products, arithmetic and copies ran while one was open for 16% of the time, Pallas kernels for 0%

profile of v1, /device:TPU:1, one launch (start us, length us, event | category | flops | bytes accessed | tf_op | source)
XLA Modules:
  0.0 246.3 jit_solution(9366353959574920145)
XLA Ops:
  7.2 4.0 %collective-permute-start.3 = (bf16[1,2,1,30,512]{4,1,3,2,0:T(2,128)(2,1)}, bf16[1,2,1,30,512]{4,1,3,2,0:T(2,128)(2,1)S(1)}, u32[]{:S(2)}, u32[]{:S(2)}) collective-permute-start(bf16[1,2,1,30,512]{4,1,3,2,0:T(2,128)(2,1)} %param.3), channel_id=1, source_target_pairs={{0,16},{16,32},{32,48},{1,17},{17,33},{33,49},{2,18},{18,34},{34,5... | collective-permute-start | bytes 184328 | tf_op jit(solution)/shard_map/ppermute | solution.py:10
  11.2 1.2 fusion.25
  12.4 4.8 %collective-permute-start = (bf16[2,1,60,256]{3,1,2,0:T(2,128)(2,1)S(1)}, bf16[2,1,60,256]{3,1,2,0:T(2,128)(2,1)S(1)}, u32[]{:S(2)}, u32[]{:S(2)}) collective-permute-start(bf16[2,1,60,256]{3,1,2,0:T(2,128)(2,1)S(1)} %get-tuple-element.46), channel_id=1, source_target_pairs={{0,1},{1,2},{2,3},{3,4},{4,5},{5,6},{6,7},{7,8},{8,9},{9,10},{10,1... | collective-permute-start | bytes 184328 | tf_op jit(solution)/shard_map/ppermute | solution.py:33
  17.2 1.3 collective-permute-start.1
  18.5 1.6 copy.102
  20.2 1.3 dynamic-slice
  22.1 1.0 pad_maximum_fusion.5
  24.2 1.6 reshape.353
  25.8 11.6 %all-to-all-start = ((bf16[16,2,1920]{2,1,0:T(2,128)(2,1)}), bf16[16,2,1920]{2,1,0:T(2,128)(2,1)S(1)}, u32[]{:S(2)}, u32[]{:S(2)}) async-start(bf16[16,2,1920]{2,1,0:T(2,128)(2,1)} %reshape.353), calls=%async_computation | async-start | bytes 245760 | tf_op jit(solution)/shard_map/all_to_all | solution.py:81
  37.9 1.7 collective-permute-start.2
  40.2 7.8 %all-to-all-done = bf16[16,2,1920]{2,1,0:T(2,128)(2,1)S(1)} async-done(((bf16[16,2,1920]{2,1,0:T(2,128)(2,1)}), bf16[16,2,1920]{2,1,0:T(2,128)(2,1)S(1)}, u32[]{:S(2)}, u32[]{:S(2)}) %all-to-all-start) | async-done | bytes 122912 | tf_op jit(solution)/shard_map/all_to_all | solution.py:81
  48.0 1.4 reshape.354
  49.4 0.9 slice_bitcast_fusion.2
  51.0 0.7 pad_slice_fusion
  51.7 0.7 copy_dynamic-update-slice_fusion.26
  52.7 0.7 copy_dynamic-update-slice_fusion.25
  53.4 0.7 copy_dynamic-update-slice_fusion.24
  54.1 0.7 copy_dynamic-update-slice_fusion.23
  54.8 0.7 copy_dynamic-update-slice_fusion.22
  55.4 0.7 copy_dynamic-update-slice_fusion.21
  56.1 0.7 copy_dynamic-update-slice_fusion.20
  56.8 0.7 copy_dynamic-update-slice_fusion.19
  57.4 0.7 copy_dynamic-update-slice_fusion.18
  58.1 0.7 copy_dynamic-update-slice_fusion.17
  58.8 1.6 pad_slice_fusion.1
  60.4 0.7 copy_dynamic-update-slice_fusion.16
  61.1 0.7 copy_dynamic-update-slice_fusion.15
  61.8 0.7 copy_dynamic-update-slice_fusion.14
  62.5 0.7 copy_dynamic-update-slice_fusion.13
  63.1 0.7 copy_dynamic-update-slice_fusion.12
  63.8 0.7 copy_dynamic-update-slice_fusion.11
  64.5 0.7 copy_dynamic-update-slice_fusion.10
  65.2 0.7 copy_dynamic-update-slice_fusion.9
  65.9 0.7 copy_dynamic-update-slice_fusion.8
  66.6 40.0 %all-gather.3.cloned.1.call-done = bf16[1,2,32,60,256]{4,1,3,0,2:T(2,128)(2,1)} async-done(((bf16[1,2,2,60,256]{4,1,3,0,2:T(2,128)(2,1)}), bf16[1,2,32,60,256]{4,1,3,0,2:T(2,128)(2,1)}) %all-gather.3.cloned.1.call-update) | async-done | bytes 1966096 | tf_op jit(solution)/shard_map/all_gather | solution.py:50
  106.6 2.9 %convert_bitcast_fusion = f32[2,32,60,256]{3,0,2,1:T(2,128)S(1)} fusion(bf16[1,2,32,60,256]{4,1,3,0,2:T(2,128)(2,1)} %all-gather.3.cloned.1.call-done), kind=kLoop, calls=%fused_computation.21 | loop fusion | flops 983040 | bytes 5898240 | tf_op jit(solution)/shard_map/convert_element_type | solution.py:85
  109.5 3.4 %pad.13 = f32[2,34,60,256]{3,0,2,1:T(2,128)} pad(f32[2,32,60,256]{3,0,2,1:T(2,128)S(1)} %convert_bitcast_fusion, f32[]{:T(128)} %constant.3.clone.1), padding=0_0x1_1x0_0x0_0 | pad | bytes 8110084 | tf_op jit(solution)/shard_map/jit(_pad)/pad | solution.py:17
  112.8 5.3 %reduce_sum.46 = f32[2,17,60,256]{3,0,2,1:T(2,128)S(1)} reduce(f32[2,17,2,60,256]{4,0,3,2,1:T(2,128)} %bitcast.115, f32[]{:T(128)} %constant.3.clone.1), dimensions={2}, to_apply=%region_1.2 | reduce | flops 522240 | bytes 6266884 | tf_op jit(solution)/shard_map/reduce_sum | solution.py:19
  118.1 16.3 %fusion.23 = (f32[2,16,60,256]{3,0,2,1:T(2,128)}, f32[2,16,1,60,256]{4,0,3,1,2:T(2,128)}, f32[2,16,1,60,256]{4,0,3,1,2:T(2,128)}, f32[2,16,60,256]{3,0,2,1:T(2,128)}) fusion(f32[2,17,60,256]{3,0,2,1:T(2,128)S(1)} %reduce_sum.46), kind=kLoop, calls=%fused_computation.89 | loop fusion | bytes 11796480 | tf_op jit(solution)/shard_map/slice | solution.py:22
  134.5 4.7 %reduce_sum.47 = f32[2,16,60,256]{3,0,2,1:T(2,128)S(1)} reduce(bf16[2,16,2,60,256]{4,0,3,2,1:T(2,128)(2,1)} %bitcast.117, f32[]{:T(128)} %constant.3.clone.1), dimensions={2}, to_apply=%region_2.3 | reduce | flops 491520 | bytes 3932164 | tf_op jit(solution)/shard_map/reduce_sum | solution.py:20
  139.2 1.9 copy.106
  141.1 1.0 copy-done.4
  142.0 5.5 %select_maximum_fusion = f32[2,16,3,62,256]{4,0,3,1,2:T(2,128)} fusion(f32[2,16,1,60,256]{4,0,3,1,2:T(2,128)S(1)} %copy-done.4, f32[2,16,1,60,256]{4,0,3,1,2:T(2,128)S(1)} %bitcast.114, f32[2,16,1,60,256]{4,0,3,1,2:T(2,128)S(1)} %copy-done.3), kind=kLoop, calls=%fused_computation.10 | loop fusion | flops 12189696 | bytes 11993088 | tf_op jit(solution)/shard_map/stack | solution.py:26
  147.5 7.7 %reduce.2 = f32[2,16,3,31,256]{4,0,3,1,2:T(2,128)S(1)} reduce(f32[2,16,3,31,2,256]{5,0,4,3,1,2:T(2,128)} %bitcast.113, f32[]{:T(128)} %constant.3.clone.1), dimensions={4}, to_apply=%region_3.4 | reduce | flops 761856 | bytes 9142276
  155.3 1.5 fusion.22
  157.5 0.9 copy-done
  159.0 0.9 maximum_reduce_fusion
  159.9 1.7 copy.159
  161.6 1.0 copy_bitcast_fusion
  162.6 2.2 fusion.1
  164.8 1.8 fusion.8
  166.6 1.1 fusion.16
  167.8 0.7 copy_dynamic-update-slice_fusion.7
  168.5 0.7 copy_dynamic-update-slice_fusion.6
  169.1 0.7 copy_dynamic-update-slice_fusion.5
  169.8 0.7 copy_dynamic-update-slice_fusion.4
  170.5 0.7 copy_dynamic-update-slice_fusion.3
  171.2 0.7 copy_dynamic-update-slice_fusion.2
  172.6 0.7 copy_dynamic-update-slice_fusion
  173.2 17.3 %reduce-scatter.3.cloned.1.call-done = f32[8,3,3,3,256]{4,0,1,3,2:T(8,128)} async-done(((f32[32,3,3,3,256]{4,0,1,3,2:T(8,128)}), f32[8,3,3,3,256]{4,0,1,3,2:T(8,128)}) %reduce-scatter.3.cloned.1.call-update) | async-done | bytes 221200 | tf_op jit(solution)/shard_map/reduce_scatter | solution.py:94
  190.6 6.1 %fusion.12 = bf16[2,30,512]{2,1,0:T(8,128)(2,1)S(1)} fusion(bf16[27,512,256,1,1,1]{2,1,0,5,4,3:T(8,128)(2,1)} %bitcast.158, bf16[2,1,2,30,2,27,256]{6,3,5,4,2,0,1:T(8,128)(2,1)} %copy_dynamic-update-slice_fusion), kind=kOutput, calls=%fused_computation.20 | convolution fusion | flops 1698785280 | bytes 10457088 | tf_op jit(solution)/shard_map/dot_general | solution.py:65
  196.7 0.7 copy.114
  197.4 40.5 %all-reduce.6.cloned.1.call-done = f32[8,3,3,3,256]{4,0,1,3,2:T(8,128)} async-done(((f32[8,3,3,3,256]{4,0,1,3,2:T(8,128)}), f32[8,3,3,3,256]{4,0,1,3,2:T(8,128)}) %all-reduce.6.cloned.1.call-update) | async-done | bytes 221200
  237.9 1.0 constant_dynamic-slice_fusion
  (47 shorter events, 5.9 us)
Async XLA Ops:
  7.2 30.3 %copy-start.5 = (bf16[1,2,2,60,256]{4,2,3,1,0:T(2,128)(2,1)S(1)}, bf16[1,2,2,60,256]{4,2,3,1,0:T(2,128)(2,1)}, u32[]{:S(2)}) copy-start(bf16[1,2,2,60,256]{4,2,3,1,0:T(2,128)(2,1)} %param.4) | copy-start | bytes 368644
  7.2 99.4 %all-gather.3.cloned.1.call-start = ((), (), s32[]{:S(2)}) async-start(), calls=%async_computation.3 | async-start | bytes 2088960 | tf_op jit(solution)/shard_map/all_gather | solution.py:50
  7.2 14.9 %collective-permute-start.3 = (bf16[1,2,1,30,512]{4,1,3,2,0:T(2,128)(2,1)}, bf16[1,2,1,30,512]{4,1,3,2,0:T(2,128)(2,1)S(1)}, u32[]{:S(2)}, u32[]{:S(2)}) collective-permute-start(bf16[1,2,1,30,512]{4,1,3,2,0:T(2,128)(2,1)} %param.3), channel_id=1, source_target_pairs={{0,16},{16,32},{32,48},{1,17},{17,33},{33,49},{2,18},{18,34},{34,5... | collective-permute-start | bytes 184328 | tf_op jit(solution)/shard_map/ppermute | solution.py:10
  12.4 25.1 %collective-permute-start = (bf16[2,1,60,256]{3,1,2,0:T(2,128)(2,1)S(1)}, bf16[2,1,60,256]{3,1,2,0:T(2,128)(2,1)S(1)}, u32[]{:S(2)}, u32[]{:S(2)}) collective-permute-start(bf16[2,1,60,256]{3,1,2,0:T(2,128)(2,1)S(1)} %get-tuple-element.46), channel_id=1, source_target_pairs={{0,1},{1,2},{2,3},{3,4},{4,5},{5,6},{6,7},{7,8},{8,9},{9,10},{10,1... | collective-permute-start | bytes 184328 | tf_op jit(solution)/shard_map/ppermute | solution.py:33
  17.2 20.3 %collective-permute-start.1 = (bf16[2,1,60,256]{3,1,2,0:T(2,128)(2,1)S(1)}, bf16[2,1,60,256]{3,1,2,0:T(2,128)(2,1)S(1)}, u32[]{:S(2)}, u32[]{:S(2)}) collective-permute-start(bf16[2,1,60,256]{3,1,2,0:T(2,128)(2,1)S(1)} %get-tuple-element.47), channel_id=1, source_target_pairs={{1,0},{2,1},{3,2},{4,3},{5,4},{6,5},{7,6},{8,7},{9,8},{10,9},{11,1... | collective-permute-start | bytes 184328 | tf_op jit(solution)/shard_map/ppermute | solution.py:36
  25.8 22.2 %all-to-all-start = ((bf16[16,2,1920]{2,1,0:T(2,128)(2,1)}), bf16[16,2,1920]{2,1,0:T(2,128)(2,1)S(1)}, u32[]{:S(2)}, u32[]{:S(2)}) async-start(bf16[16,2,1920]{2,1,0:T(2,128)(2,1)} %reshape.353), calls=%async_computation | async-start | bytes 245760 | tf_op jit(solution)/shard_map/all_to_all | solution.py:81
  37.4 153.1 %reduce-scatter.3.cloned.1.call-start = ((), (), s32[]{:S(2)}) async-start(), calls=%async_computation.2 | async-start | bytes 1105920 | tf_op jit(solution)/shard_map/reduce_scatter | solution.py:94
  37.9 12.4 %collective-permute-start.2 = (bf16[2,4,60,256]{3,1,2,0:T(4,128)(2,1)S(1)}, bf16[2,4,60,256]{3,1,2,0:T(4,128)(2,1)S(1)}, u32[]{:S(2)}, u32[]{:S(2)}) collective-permute-start(bf16[2,4,60,256]{3,1,2,0:T(4,128)(2,1)S(1)} %pad_maximum_fusion.2), channel_id=1, source_target_pairs={{16,0},{32,16},{48,32},{17,1},{33,17},{49,33},{18,2},{34,18},{50,3... | collective-permute-start | bytes 737288 | tf_op jit(solution)/shard_map/ppermute | solution.py:10
  139.2 1.9 copy-start.3
  139.2 2.8 %copy-start.4 = (f32[2,16,1,60,256]{4,0,3,1,2:T(2,128)S(1)}, f32[2,16,1,60,256]{4,0,3,1,2:T(2,128)}, u32[]{:S(2)}) copy-start(f32[2,16,1,60,256]{4,0,3,1,2:T(2,128)} %get-tuple-element.16) | copy-start | bytes 5898244
  155.3 1.6 copy-start.1
  156.8 1.5 copy-start
  156.8 2.2 copy-start.2
  162.5 2.3 copy-start.10
  162.5 2.3 copy-start.11
  162.6 2.3 copy-start.12
  166.6 1.9 copy-start.9
  166.6 2.5 %copy-start.8 = (bf16[2,2,60,256]{3,1,2,0:T(2,128)(2,1)S(1)}, bf16[2,2,60,256]{3,1,2,0:T(2,128)(2,1)}, u32[]{:S(2)}) copy-start(bf16[2,2,60,256]{3,1,2,0:T(2,128)(2,1)} %get-tuple-element.37) | copy-start | bytes 368644
  166.6 3.9 %copy-start.7 = (bf16[2,2,60,256]{3,1,2,0:T(2,128)(2,1)S(1)}, bf16[2,2,60,256]{3,1,2,0:T(2,128)(2,1)}, u32[]{:S(2)}) copy-start(bf16[2,2,60,256]{3,1,2,0:T(2,128)(2,1)} %get-tuple-element.38) | copy-start | bytes 368644
  166.6 4.6 %copy-start.6 = (bf16[2,2,60,256]{3,1,2,0:T(2,128)(2,1)S(1)}, bf16[2,2,60,256]{3,1,2,0:T(2,128)(2,1)}, u32[]{:S(2)}) copy-start(bf16[2,2,60,256]{3,1,2,0:T(2,128)(2,1)} %get-tuple-element.31) | copy-start | bytes 368644
  167.7 70.2 %all-reduce.6.cloned.1.call-start = ((), (), s32[]{:S(2)}) async-start(), calls=%async_computation.4 | async-start | bytes 442368
Sparse Core Ops, SparseCore 0:
  20.3 86.2 all-gather.2
  167.8 22.6 reduce-scatter.2
  192.9 44.9 all-reduce.5

commit v2 on v1

--- a/solution.py
+++ b/solution.py
@@ -2,6 +2,8 @@
 import jax.numpy as jnp
 from jax import lax
 from jax.sharding import PartitionSpec as P
+from jax.experimental import pallas as pl
+from jax.experimental.pallas import tpu as pltpu
 
 
 def shift_from(shard, axis, by):
@@ -35,6 +37,68 @@
     )
     high = lax.ppermute(lax.slice_in_dim(block, 0, width, axis=dim), axis, backward)
     return jnp.concatenate([low, block, high], axis=dim)
+
+
+def scatter_sum_kernel(term_ref, out_ref, slots, send_sem, recv_sem):
+    tm_size = lax.axis_size("tm")
+    count = lax.axis_size("dp") * tm_size
+    row = lax.axis_index("rows")
+    me = lax.axis_index("dp") * tm_size + lax.axis_index("tm")
+    mesh_id = pl.DeviceIdType.MESH
+
+    def device(k):
+        return (k // tm_size, k % tm_size, row)
+
+    barrier = pltpu.get_barrier_semaphore()
+    for d in range(1, count):
+        pl.semaphore_signal(barrier, inc=1, device_id=device((me + d) % count), device_id_type=mesh_id)
+    pl.semaphore_wait(barrier, count - 1)
+
+    copies = []
+    for d in range(1, count):
+        target = (me + d) % count
+        copy = pltpu.make_async_remote_copy(
+            src_ref=term_ref.at[target],
+            dst_ref=slots.at[me],
+            send_sem=send_sem.at[d - 1],
+            recv_sem=recv_sem.at[me],
+            device_id=device(target),
+            device_id_type=mesh_id,
+        )
+        copy.start()
+        copies.append(copy)
+    total = term_ref[me]
+    for d in range(1, count):
+        source = (me + count - d) % count
+        incoming = pltpu.make_async_remote_copy(
+            src_ref=term_ref.at[source],
+            dst_ref=slots.at[source],
+            send_sem=send_sem.at[d - 1],
+            recv_sem=recv_sem.at[source],
+            device_id=device(source),
+            device_id_type=mesh_id,
+        )
+        incoming.wait_recv()
+        total = total + slots[source]
+    out_ref[...] = total
+    for copy in copies:
+        copy.wait_send()
+
+
+def scatter_sum(term):
+    count, rows, lanes = term.shape
+    return pl.pallas_call(
+        scatter_sum_kernel,
+        out_shape=jax.ShapeDtypeStruct((rows, lanes), term.dtype),
+        in_specs=[pl.BlockSpec(memory_space=pltpu.VMEM)],
+        out_specs=pl.BlockSpec(memory_space=pltpu.VMEM),
+        scratch_shapes=[
+            pltpu.VMEM((count, rows, lanes), term.dtype),
+            pltpu.SemaphoreType.DMA((count - 1,)),
+            pltpu.SemaphoreType.DMA((count,)),
+        ],
+        compiler_params=pltpu.CompilerParams(collective_id=0, has_side_effects=True),
+    )(term)
 
 
 def body(latents, grad_out, kernel):
@@ -90,9 +154,9 @@
         "afrsc,xfrisjo->caijxo", taps_a, both, preferred_element_type=jnp.float32
     )
     term = (term[..., 0, :] + term[..., 1, :]) * factor
-    term = term.reshape(group_channels, 3, 3, 3, outputs)
-    term = lax.psum_scatter(term, "dp", scatter_dimension=0, tiled=True)
-    weight_grad = lax.psum_scatter(term, "tm", scatter_dimension=0, tiled=True)
+    share_size = share * 27 * outputs
+    term = term.reshape(groups, share_size // 128, 128)
+    weight_grad = scatter_sum(term).reshape(share, 3, 3, 3, outputs)
     return (grad_latents, weight_grad)
 
 

time: 251 us -> 202 us (0.80)
  waiting for transfers between devices: 106 us -> 59.8 us
  local copies, waits for them, and re-layouts: 61.5 us -> 31.4 us
  Pallas kernels: 0 us -> 20.5 us
  other arithmetic: 32.8 us -> 44.2 us
  matrix products: 7.87 us -> 3.79 us
    unnamed x4 -> x1, waiting for transfers between devices: 40.6 us -> 0.02 us
    pallas_call x0 -> x1, Pallas kernels: none -> 20.5 us  [scatter_sum(): pl.pallas_call(scatter_sum_kernel, out_shape=jax.ShapeDtypeStruct((rows,...]
    unnamed x59 -> x51, local copies, waits for them, and re-layouts: 27.8 us -> 8.4 us
    reduce_scatter x1 -> x0, waiting for transfers between devices: 17.3 us -> none  [body(): term = lax.psum_scatter(term, 'dp', scatter_dimension=0, tiled=True)]
    all_gather x1, waiting for transfers between devices: 40 us -> 52.6 us  [body(): grad_whole = lax.all_gather(grad_out[0], 'rows', axis=1, tiled=True)]
    reduce_sum x1, other arithmetic: 5.32 us -> 17.6 us  [pool_pairs(): ext.reshape(shape[:dim] + (n + 1, 2) + shape[dim + 1:]).sum(axis=dim + 1)]
    slice x3, local copies, waits for them, and re-layouts: 18.5 us -> 6.43 us  [pool_pairs(): lax.slice_in_dim(shifted, 1, n + 1, axis=dim)]
    dot_general x1, matrix products: 6.12 us -> 2.03 us  [body(): lax.dot_general(patches, kernel.reshape(27, channels, outputs), (((1, 2),...]
  transfers between devices with their start and end apart: 8 -> 6, of which waited for: 4 -> 2; matrix products, arithmetic and copies ran while one was open for 16% -> 8% of each run, Pallas kernels for 0% -> 0%
where the time goes in v2:
time: 202 us; the launch traced here: 198 us
  waiting for transfers between devices  59.8 us (30%)
  other arithmetic  44.2 us (22%)
  local copies, waits for them, and re-layouts  31.4 us (16%)
  starting transfers between devices  23.4 us (12%)
  Pallas kernels  20.5 us (10%)
  between operations  14.8 us (7%)
  matrix products  3.79 us (2%)
    all_gather x1, waiting for transfers between devices, body(): grad_whole = lax.all_gather(grad_out[0], 'rows', axis=1, tiled=True)  52.6 us
    pallas_call x1, Pallas kernels, scatter_sum(): pl.pallas_call(scatter_sum_kernel, out_shape=jax.ShapeDtypeStruct((rows,...  20.5 us
    reduce_sum x1, other arithmetic, pool_pairs(): ext.reshape(shape[:dim] + (n + 1, 2) + shape[dim + 1:]).sum(axis=dim + 1)  17.6 us
    all_to_all x1, starting transfers between devices, body(): lax.all_to_all(regrouped, 'rows', split_axis=4, concat_axis=2, tiled=True)  11.6 us
    unnamed x51, local copies, waits for them, and re-layouts  8.4 us
    unnamed x2, other arithmetic  7.74 us
    all_to_all x1, waiting for transfers between devices, body(): lax.all_to_all(regrouped, 'rows', split_axis=4, concat_axis=2, tiled=True)  7.22 us
    slice x3, local copies, waits for them, and re-layouts, pool_pairs(): lax.slice_in_dim(shifted, 1, n + 1, axis=dim)  6.43 us
  transfers between devices with their start and end apart: 6, of which 2 were waited for; matrix products, arithmetic and copies ran while one was open for 8% of the time, Pallas kernels for 0%

profile of v2, /device:TPU:1, one launch (start us, length us, event | category | flops | bytes accessed | tf_op | source)
XLA Modules:
  0.0 197.9 jit_solution(4135856965386165395)
XLA Ops:
  7.2 0.0 copy-start.5
  7.2 0.0 all-gather.3.cloned.1.call-start
  7.2 4.0 %collective-permute-start.3 = (bf16[1,2,1,30,512]{4,1,3,2,0:T(2,128)(2,1)}, bf16[1,2,1,30,512]{4,1,3,2,0:T(2,128)(2,1)S(1)}, u32[]{:S(2)}, u32[]{:S(2)}) collective-permute-start(bf16[1,2,1,30,512]{4,1,3,2,0:T(2,128)(2,1)} %param.3), channel_id=1, source_target_pairs={{0,16},{16,32},{32,48},{1,17},{17,33},{33,49},{2,18},{18,34},{34,5... | collective-permute-start | bytes 184328 | tf_op jit(solution)/shard_map/ppermute | solution.py:12
  11.2 1.2 fusion.24
  12.4 4.8 %collective-permute-start = (bf16[2,1,60,256]{3,1,2,0:T(2,128)(2,1)S(1)}, bf16[2,1,60,256]{3,1,2,0:T(2,128)(2,1)S(1)}, u32[]{:S(2)}, u32[]{:S(2)}) collective-permute-start(bf16[2,1,60,256]{3,1,2,0:T(2,128)(2,1)S(1)} %get-tuple-element.46), channel_id=1, source_target_pairs={{0,1},{1,2},{2,3},{3,4},{4,5},{5,6},{6,7},{7,8},{8,9},{9,10},{10,1... | collective-permute-start | bytes 184328 | tf_op jit(solution)/shard_map/ppermute | solution.py:35
  17.2 1.3 collective-permute-start.1
  18.5 1.6 copy.105
  20.2 0.0 all-gather.3.cloned.1.call-update
  20.2 0.0 collective-permute-done.3
  20.2 1.0 pad_maximum_fusion.5
  21.2 0.3 copy.113
  21.5 0.4 copy.114
  21.9 0.4 copy.162
  22.3 1.7 reshape.357
  23.9 11.6 %all-to-all-start = ((bf16[16,2,1920]{2,1,0:T(2,128)(2,1)}), bf16[16,2,1920]{2,1,0:T(2,128)(2,1)S(1)}, u32[]{:S(2)}, u32[]{:S(2)}) async-start(bf16[16,2,1920]{2,1,0:T(2,128)(2,1)} %reshape.357), calls=%async_computation | async-start | bytes 245760 | tf_op jit(solution)/shard_map/all_to_all | solution.py:145
  35.5 0.0 collective-permute-done
  35.6 0.0 collective-permute-done.1
  35.6 0.4 pad_maximum_fusion.2
  36.0 1.7 collective-permute-start.2
  37.7 0.5 pad_maximum_fusion.3
  38.2 7.2 %all-to-all-done = bf16[16,2,1920]{2,1,0:T(2,128)(2,1)S(1)} async-done(((bf16[16,2,1920]{2,1,0:T(2,128)(2,1)}), bf16[16,2,1920]{2,1,0:T(2,128)(2,1)S(1)}, u32[]{:S(2)}, u32[]{:S(2)}) %all-to-all-start) | async-done | bytes 122912 | tf_op jit(solution)/shard_map/all_to_all | solution.py:145
  45.5 1.4 reshape.358
  46.8 0.0 slice-start
  46.8 0.1 copy.116
  46.9 0.9 slice_bitcast_fusion.2
  47.8 0.0 collective-permute-done.2
  47.8 0.5 pad_maximum_fusion.1
  48.3 0.2 pad_slice_fusion.17
  48.5 0.7 pad_slice_fusion
  49.2 0.0 slice-start.1
  49.2 0.7 pad_slice_fusion.1
  50.0 0.3 fusion.23
  50.9 0.0 slice-done
  50.9 0.1 slice-done.1
  51.0 2.0 %fusion.12 = bf16[2,30,512]{2,1,0:T(8,128)(2,1)S(1)} fusion(bf16[27,512,256,1,1,1]{2,1,0,5,4,3:T(8,128)(2,1)S(1)} %bitcast.157, bf16[2,1,2,30,2,27,256]{6,3,5,4,2,0,1:T(8,128)(2,1)S(1)} %copy_dynamic-update-slice_fusion), kind=kOutput, calls=%fused_computation.20 | convolution fusion | flops 1698785280 | bytes 10457088 | tf_op jit(solution)/shard_map/dot_general | solution.py:129
  53.1 0.7 copy.118
  53.8 52.6 %all-gather.3.cloned.1.call-done = bf16[1,2,32,60,256]{4,1,3,0,2:T(2,128)(2,1)} async-done(((bf16[1,2,2,60,256]{4,1,3,0,2:T(2,128)(2,1)}), bf16[1,2,32,60,256]{4,1,3,0,2:T(2,128)(2,1)}) %all-gather.3.cloned.1.call-update) | async-done | bytes 1966096 | tf_op jit(solution)/shard_map/all_gather | solution.py:114
  106.3 2.9 %convert_bitcast_fusion = f32[2,32,60,256]{3,0,2,1:T(2,128)S(1)} fusion(bf16[1,2,32,60,256]{4,1,3,0,2:T(2,128)(2,1)} %all-gather.3.cloned.1.call-done), kind=kLoop, calls=%fused_computation.21 | loop fusion | flops 983040 | bytes 5898240 | tf_op jit(solution)/shard_map/convert_element_type | solution.py:149
  109.2 3.4 %pad.13 = f32[2,34,60,256]{3,0,2,1:T(2,128)} pad(f32[2,32,60,256]{3,0,2,1:T(2,128)S(1)} %convert_bitcast_fusion, f32[]{:T(128)} %constant.3.clone.1), padding=0_0x1_1x0_0x0_0 | pad | bytes 8110084 | tf_op jit(solution)/shard_map/jit(_pad)/pad | solution.py:19
  112.6 17.6 %reduce_sum.46 = f32[2,17,60,256]{3,0,2,1:T(2,128)S(1)} reduce(f32[2,17,2,60,256]{4,0,3,2,1:T(2,128)} %bitcast.112, f32[]{:T(128)} %constant.3.clone.1), dimensions={2}, to_apply=%region_1.2 | reduce | flops 522240 | bytes 6266884 | tf_op jit(solution)/shard_map/reduce_sum | solution.py:21
  130.3 4.3 %fusion.22 = (f32[2,16,60,256]{3,0,2,1:T(2,128)}, f32[2,16,1,60,256]{4,0,3,1,2:T(2,128)}, f32[2,16,1,60,256]{4,0,3,1,2:T(2,128)}, f32[2,16,60,256]{3,0,2,1:T(2,128)}) fusion(f32[2,17,60,256]{3,0,2,1:T(2,128)S(1)} %reduce_sum.46), kind=kLoop, calls=%fused_computation.87 | loop fusion | bytes 11796480 | tf_op jit(solution)/shard_map/slice | solution.py:24
  134.5 4.7 %reduce_sum.47 = f32[2,16,60,256]{3,0,2,1:T(2,128)S(1)} reduce(bf16[2,16,2,60,256]{4,0,3,2,1:T(2,128)(2,1)} %bitcast.114, f32[]{:T(128)} %constant.3.clone.1), dimensions={2}, to_apply=%region_2.3 | reduce | flops 491520 | bytes 3932164 | tf_op jit(solution)/shard_map/reduce_sum | solution.py:22
  139.3 1.9 copy.109
  141.2 0.9 copy-done.4
  142.1 5.5 %select_maximum_fusion = f32[2,16,3,62,256]{4,0,3,1,2:T(2,128)} fusion(f32[2,16,1,60,256]{4,0,3,1,2:T(2,128)S(1)} %copy-done.4, f32[2,16,1,60,256]{4,0,3,1,2:T(2,128)S(1)} %bitcast.111, f32[2,16,1,60,256]{4,0,3,1,2:T(2,128)S(1)} %copy-done.3), kind=kLoop, calls=%fused_computation.10 | loop fusion | flops 12189696 | bytes 11993088 | tf_op jit(solution)/shard_map/stack | solution.py:28
  147.6 7.7 %reduce.2 = f32[2,16,3,31,256]{4,0,3,1,2:T(2,128)S(1)} reduce(f32[2,16,3,31,2,256]{5,0,4,3,1,2:T(2,128)} %bitcast.110, f32[]{:T(128)} %constant.3.clone.1), dimensions={4}, to_apply=%region_3.4 | reduce | flops 761856 | bytes 9142276
  155.4 0.0 copy-start.1
  155.4 1.5 fusion.21
  156.9 0.0 copy-start
  156.9 0.0 copy-done.1
  157.0 0.6 copy.108
  157.6 0.9 copy-done
  158.5 0.6 copy.110
  159.1 0.9 maximum_reduce_fusion
  160.0 1.7 copy.161
  161.7 1.0 copy_bitcast_fusion
  162.7 2.2 %fusion.1 = (bf16[1,2,16,3,30,3,256]{6,4,2,1,5,3,0:T(8,128)(2,1)S(1)}, bf16[1,2,16,3,30,3,256]{6,4,2,1,5,3,0:T(8,128)(2,1)S(1)}) fusion(f32[1,2,16,3,30,1,256]{6,4,2,1,5,3,0:T(8,128)S(1)} %get-tuple-element.48, f32[1,2,16,3,30,1,256]{6,4,2,1,5,3,0:T(8,128)S(1)} %bitcast.113, f32[1,2,16,3,30,1,256]{6,4,2,1,5,3,0:T(8,128)S(1)} %get-tuple-element.49), kind=kLoop, calls=%fused_computation.2 | loop fusion | flops 17694720 | bytes 17694720 | tf_op jit(solution)/shard_map/convert
  164.9 1.8 fusion.8
  166.7 0.1 fusion.15
  166.8 0.6 copy.117
  167.4 1.4 mul.31.term_ref
  168.8 20.5 %shard_map.50 = f32[108,128]{1,0:T(8,128)} custom-call(f32[16,108,128]{2,1,0:T(8,128)} %mul.31.term_ref), custom_call_target="tpu_custom_call" | custom-call | tf_op jit(solution)/shard_map/pallas_call | solution.py:90
  189.4 0.8 reshape.348
  190.2 0.7 copy.119
  (38 shorter events, 0.5 us)
Async XLA Ops:
  7.2 28.4 %copy-start.5 = (bf16[1,2,2,60,256]{4,2,3,1,0:T(2,128)(2,1)S(1)}, bf16[1,2,2,60,256]{4,2,3,1,0:T(2,128)(2,1)}, u32[]{:S(2)}) copy-start(bf16[1,2,2,60,256]{4,2,3,1,0:T(2,128)(2,1)} %param.4) | copy-start | bytes 368644
  7.2 99.1 %all-gather.3.cloned.1.call-start = ((), (), s32[]{:S(2)}) async-start(), calls=%async_computation.1 | async-start | bytes 2088960 | tf_op jit(solution)/shard_map/all_gather | solution.py:114
  7.2 13.0 %collective-permute-start.3 = (bf16[1,2,1,30,512]{4,1,3,2,0:T(2,128)(2,1)}, bf16[1,2,1,30,512]{4,1,3,2,0:T(2,128)(2,1)S(1)}, u32[]{:S(2)}, u32[]{:S(2)}) collective-permute-start(bf16[1,2,1,30,512]{4,1,3,2,0:T(2,128)(2,1)} %param.3), channel_id=1, source_target_pairs={{0,16},{16,32},{32,48},{1,17},{17,33},{33,49},{2,18},{18,34},{34,5... | collective-permute-start | bytes 184328 | tf_op jit(solution)/shard_map/ppermute | solution.py:12
  12.4 23.2 %collective-permute-start = (bf16[2,1,60,256]{3,1,2,0:T(2,128)(2,1)S(1)}, bf16[2,1,60,256]{3,1,2,0:T(2,128)(2,1)S(1)}, u32[]{:S(2)}, u32[]{:S(2)}) collective-permute-start(bf16[2,1,60,256]{3,1,2,0:T(2,128)(2,1)S(1)} %get-tuple-element.46), channel_id=1, source_target_pairs={{0,1},{1,2},{2,3},{3,4},{4,5},{5,6},{6,7},{7,8},{8,9},{9,10},{10,1... | collective-permute-start | bytes 184328 | tf_op jit(solution)/shard_map/ppermute | solution.py:35
  17.2 18.3 %collective-permute-start.1 = (bf16[2,1,60,256]{3,1,2,0:T(2,128)(2,1)S(1)}, bf16[2,1,60,256]{3,1,2,0:T(2,128)(2,1)S(1)}, u32[]{:S(2)}, u32[]{:S(2)}) collective-permute-start(bf16[2,1,60,256]{3,1,2,0:T(2,128)(2,1)S(1)} %get-tuple-element.47), channel_id=1, source_target_pairs={{1,0},{2,1},{3,2},{4,3},{5,4},{6,5},{7,6},{8,7},{9,8},{10,9},{11,1... | collective-permute-start | bytes 184328 | tf_op jit(solution)/shard_map/ppermute | solution.py:38
  23.9 21.5 %all-to-all-start = ((bf16[16,2,1920]{2,1,0:T(2,128)(2,1)}), bf16[16,2,1920]{2,1,0:T(2,128)(2,1)S(1)}, u32[]{:S(2)}, u32[]{:S(2)}) async-start(bf16[16,2,1920]{2,1,0:T(2,128)(2,1)} %reshape.357), calls=%async_computation | async-start | bytes 245760 | tf_op jit(solution)/shard_map/all_to_all | solution.py:145
  36.0 11.8 %collective-permute-start.2 = (bf16[2,4,60,256]{3,1,2,0:T(4,128)(2,1)S(1)}, bf16[2,4,60,256]{3,1,2,0:T(4,128)(2,1)S(1)}, u32[]{:S(2)}, u32[]{:S(2)}) collective-permute-start(bf16[2,4,60,256]{3,1,2,0:T(4,128)(2,1)S(1)} %pad_maximum_fusion.2), channel_id=1, source_target_pairs={{16,0},{32,16},{48,32},{17,1},{33,17},{49,33},{18,2},{34,18},{50,3... | collective-permute-start | bytes 737288 | tf_op jit(solution)/shard_map/ppermute | solution.py:12
  46.8 4.1 %slice-start = ((s8[7077888]{0:T(1024)(128)(4,1)}), s8[4194304]{0:T(1024)(128)(4,1)S(1)}, s32[]{:S(2)}) async-start(s8[7077888]{0:T(1024)(128)(4,1)} %bitcast.155), calls=%async_computation.2 | async-start | bytes 8388608
  49.2 1.8 slice-start.1
  139.3 1.9 copy-start.3
  139.3 2.8 %copy-start.4 = (f32[2,16,1,60,256]{4,0,3,1,2:T(2,128)S(1)}, f32[2,16,1,60,256]{4,0,3,1,2:T(2,128)}, u32[]{:S(2)}) copy-start(f32[2,16,1,60,256]{4,0,3,1,2:T(2,128)} %get-tuple-element.16) | copy-start | bytes 5898244
  155.4 1.6 copy-start.1
  156.9 1.5 copy-start
  157.0 2.2 %copy-start.2 = (f32[2,16,60,256]{3,1,2,0:T(8,128)S(1)}, f32[2,16,60,256]{3,1,2,0:T(8,128)}, u32[]{:S(2)}) copy-start(f32[2,16,60,256]{3,1,2,0:T(8,128)} %copy.109) | copy-start | bytes 5898244
  162.7 2.3 %copy-start.6 = (bf16[1,2,16,30,32]{3,4,2,1,0:T(8,128)(2,1)S(1)}, bf16[1,2,16,30,32]{3,4,2,1,0:T(8,128)(2,1)}, u32[]{:S(2)}) copy-start(bf16[1,2,16,30,32]{3,4,2,1,0:T(8,128)(2,1)} %get-tuple-element.19) | copy-start | bytes 184324
  162.7 2.3 %copy-start.7 = (bf16[1,2,16,30,32]{3,4,2,1,0:T(8,128)(2,1)S(1)}, bf16[1,2,16,30,32]{3,4,2,1,0:T(8,128)(2,1)}, u32[]{:S(2)}) copy-start(bf16[1,2,16,30,32]{3,4,2,1,0:T(8,128)(2,1)} %get-tuple-element.20) | copy-start | bytes 184324
Sparse Core Ops, SparseCore 0:
  20.3 85.9 all-gather.2

commit v3 on v2

--- a/solution.py
+++ b/solution.py
@@ -101,6 +101,73 @@
     )(term)
 
 
+def row_exchange_kernel(grad_ref, lat_ref, grad_buf, lat_buf, send_sem, recv_sem):
+    count = lax.axis_size("rows")
+    me = lax.axis_index("rows")
+    mesh_id = pl.DeviceIdType.MESH
+
+    def device(k):
+        return (lax.axis_index("dp"), lax.axis_index("tm"), k)
+
+    barrier = pltpu.get_barrier_semaphore()
+    for d in range(1, count):
+        pl.semaphore_signal(barrier, inc=1, device_id=device((me + d) % count), device_id_type=mesh_id)
+    pl.semaphore_wait(barrier, count - 1)
+
+    def grad_copy(d, peer, slot):
+        return pltpu.make_async_remote_copy(
+            src_ref=grad_ref,
+            dst_ref=grad_buf.at[slot],
+            send_sem=send_sem.at[0, d - 1],
+            recv_sem=recv_sem.at[0, slot],
+            device_id=device(peer),
+            device_id_type=mesh_id,
+        )
+
+    def lat_copy(d, peer, chunk, slot):
+        return pltpu.make_async_remote_copy(
+            src_ref=lat_ref.at[chunk],
+            dst_ref=lat_buf.at[slot],
+            send_sem=send_sem.at[1, d - 1],
+            recv_sem=recv_sem.at[1, slot],
+            device_id=device(peer),
+            device_id_type=mesh_id,
+        )
+
+    copies = []
+    for d in range(1, count):
+        target = (me + d) % count
+        for copy in (lat_copy(d, target, target, me), grad_copy(d, target, me)):
+            copy.start()
+            copies.append(copy)
+    grad_buf[me] = grad_ref[...]
+    lat_buf[me] = lat_ref[me]
+    for d in range(1, count):
+        source = (me + count - d) % count
+        lat_copy(d, source, source, source).wait_recv()
+        grad_copy(d, source, source).wait_recv()
+    for copy in copies:
+        copy.wait_send()
+
+
+def row_exchange(grad_send, lat_send):
+    count = lat_send.shape[0]
+    return pl.pallas_call(
+        row_exchange_kernel,
+        out_shape=(
+            jax.ShapeDtypeStruct((count,) + grad_send.shape, grad_send.dtype),
+            jax.ShapeDtypeStruct(lat_send.shape, lat_send.dtype),
+        ),
+        in_specs=[pl.BlockSpec(memory_space=pltpu.VMEM)] * 2,
+        out_specs=(pl.BlockSpec(memory_space=pltpu.VMEM),) * 2,
+        scratch_shapes=[
+            pltpu.SemaphoreType.DMA((2, count - 1)),
+            pltpu.SemaphoreType.DMA((2, count)),
+        ],
+        compiler_params=pltpu.CompilerParams(collective_id=1, has_side_effects=True),
+    )(grad_send, lat_send)
+
+
 def body(latents, grad_out, kernel):
     frames = grad_out.shape[1]
     height = grad_out.shape[2]
@@ -110,9 +177,6 @@
     devices = lax.axis_size("dp") * lax.axis_size("tm") * lax.axis_size("rows")
     factor = float(devices * frames * height * width) ** (-0.5)
     slab_count = lax.axis_size("rows")
-
-    grad_whole = lax.all_gather(grad_out[0], "rows", axis=1, tiled=True)
-    whole_height = grad_whole.shape[1]
 
     near = with_halo(grad_out[0], "rows", 1, 1)
     later = shift_from(near, "tm", -1)
@@ -138,20 +202,44 @@
     groups = lax.axis_size("dp") * lax.axis_size("tm")
     share = channels // devices
     earlier = shift_from(latents, "tm", 1)
-    with_earlier = jnp.concatenate([earlier, latents], axis=1)
-    lead = with_earlier.shape[:4]
+    with_earlier = jnp.concatenate([earlier, latents], axis=1)[0, :, 0]
+    lead = with_earlier.shape[:2]
     regrouped = with_earlier.reshape(lead + (groups, slab_count, share))
-    regrouped = jnp.swapaxes(regrouped, 4, 5).reshape(lead + (channels,))
-    owned = lax.all_to_all(regrouped, "rows", split_axis=4, concat_axis=2, tiled=True)[0]
-    group_channels = owned.shape[3]
-    taps_a = jnp.stack([owned[a : a + frames] for a in range(3)], axis=0)
-
-    pooled_grad = pool_pairs(pool_pairs(grad_whole.astype(jnp.float32), 1), 3)
+    regrouped = jnp.transpose(regrouped, (3, 0, 1, 2, 4))
+    lat_send = regrouped.reshape(slab_count, -1, 128)
+    grad_send = grad_out[0].reshape(frames * height * (width // 2), 2 * outputs)
+    grad_buf, lat_buf = row_exchange(grad_send, lat_send)
+    group_channels = groups * share
+    owned = lat_buf.reshape(slab_count, lead[0], width // 2, group_channels)
+    taps_a = jnp.stack([owned[:, a : a + frames] for a in range(3)], axis=0)
+
+    whole = grad_buf.reshape(slab_count, frames, height, width // 2, 2 * outputs)
+    whole = whole.astype(jnp.float32)
+    top_row, bottom_row = whole[:, :, 0], whole[:, :, 1]
+    zero = jnp.zeros_like(top_row[:1])
+    rows_pooled = jnp.stack(
+        [
+            bottom_row + jnp.concatenate([top_row[1:], zero], axis=0),
+            top_row + bottom_row,
+            top_row + jnp.concatenate([zero, bottom_row[:-1]], axis=0),
+        ],
+        axis=2,
+    )
+    left, right = rows_pooled[..., :outputs], rows_pooled[..., outputs:]
+    zero = jnp.zeros_like(left[:, :, :, :1])
+    pooled_grad = jnp.stack(
+        [
+            right + jnp.concatenate([left[:, :, :, 1:], zero], axis=3),
+            left + right,
+            left + jnp.concatenate([zero, right[:, :, :, :-1]], axis=3),
+        ],
+        axis=4,
+    )
     scaled = pooled_grad * 65537.0
     top = scaled - (scaled - pooled_grad)
     both = jnp.stack([top, pooled_grad - top], axis=0).astype(jnp.bfloat16)
     term = jnp.einsum(
-        "afrsc,xfrisjo->caijxo", taps_a, both, preferred_element_type=jnp.float32
+        "arfsc,xrfisjo->caijxo", taps_a, both, preferred_element_type=jnp.float32
     )
     term = (term[..., 0, :] + term[..., 1, :]) * factor
     share_size = share * 27 * outputs

time: 202 us -> 140 us (0.69); the launches traced: 198 us -> 140 us
  waiting for transfers between devices: 59.8 us -> 0.01 us
  Pallas kernels: 20.5 us -> 78.7 us
  other arithmetic: 44.2 us -> 17.3 us
  between operations: 14.8 us -> 1.12 us
  starting transfers between devices: 23.4 us -> 11.4 us
  local copies, waits for them, and re-layouts: 31.4 us -> 24.5 us
  matrix products: 3.79 us -> 6.78 us
    pallas_call x0 -> x1, Pallas kernels: none -> 57.9 us  [row_exchange(): pl.pallas_call(row_exchange_kernel, out_shape=(jax.ShapeDtypeStruct((coun...]
    all_gather x1 -> x0, waiting for transfers between devices: 52.6 us -> none  [body(): grad_whole = lax.all_gather(grad_out[0], 'rows', axis=1, tiled=True)]
    reduce_sum x3 -> x0, other arithmetic: 23.2 us -> none  [the longest x1 17.6 us: pool_pairs(): ext.reshape(shape[:dim] + (n + 1, 2) + shape[dim + 1:]).sum(axis=dim + 1)]
    all_to_all x1 -> x0, starting transfers between devices: 11.6 us -> none  [body(): lax.all_to_all(regrouped, 'rows', split_axis=4, concat_axis=2, tiled=True)]
    unnamed x2 -> x0, other arithmetic: 7.74 us -> none
    all_to_all x1 -> x0, waiting for transfers between devices: 7.22 us -> none  [body(): lax.all_to_all(regrouped, 'rows', split_axis=4, concat_axis=2, tiled=True)]
    another operation x2 -> x5, other arithmetic: 7.76 us -> 12.6 us  [the longest x1 6.19 us: body(): jnp.stack([right + jnp.concatenate([left[:, :, :, 1:], zero], axis=3), le...]
    unnamed x51 -> x38, local copies, waits for them, and re-layouts: 8.4 us -> 4.31 us
  transfers between devices with their start and end apart: 6 -> 4, of which waited for: 2 -> 0; matrix products, arithmetic and copies ran while one was open for 8% -> 28% of each run, Pallas kernels for 0% -> 56%
where the time goes in v3:
time: 140 us
  Pallas kernels  78.7 us (56%)
  local copies, waits for them, and re-layouts  24.5 us (18%)
  other arithmetic  17.3 us (12%)
  starting transfers between devices  11.4 us (8%)
  matrix products  6.78 us (5%)
    pallas_call x1, Pallas kernels, row_exchange(): pl.pallas_call(row_exchange_kernel, out_shape=(jax.ShapeDtypeStruct((coun...  57.9 us
    pallas_call x1, Pallas kernels, scatter_sum(): pl.pallas_call(scatter_sum_kernel, out_shape=jax.ShapeDtypeStruct((rows,...  20.8 us
    another operation x1, other arithmetic, body(): jnp.stack([right + jnp.concatenate([left[:, :, :, 1:], zero], axis=3), le...  6.19 us
    ppermute x2, starting transfers between devices, shift_from(): return lax.ppermute(shard, axis, pairs)  5.24 us
    dot_general x1, matrix products, body(): lax.dot_general(patches, kernel.reshape(27, channels, outputs), (((1, 2),...  5.04 us
    ppermute x1, starting transfers between devices, with_halo(): lax.ppermute(lax.slice_in_dim(block, block.shape[dim] - width, None, axis...  4.83 us
    unnamed x38, local copies, waits for them, and re-layouts  4.31 us
    slice x1, local copies, waits for them, and re-layouts, body(): left[:, :, :, 1:]  4.06 us
  transfers between devices with their start and end apart: 4, of which 0 were waited for; matrix products, arithmetic and copies ran while one was open for 28% of the time, Pallas kernels for 56%

profile of v3, /device:TPU:1, one launch (start us, length us, event | category | flops | bytes accessed | tf_op | source)
XLA Modules:
  0.0 139.7 jit_solution(17556087218659080057)
XLA Ops:
  0.6 4.0 %collective-permute-start.3 = (bf16[1,2,1,30,512]{4,1,3,2,0:T(2,128)(2,1)}, bf16[1,2,1,30,512]{4,1,3,2,0:T(2,128)(2,1)S(1)}, u32[]{:S(2)}, u32[]{:S(2)}) collective-permute-start(bf16[1,2,1,30,512]{4,1,3,2,0:T(2,128)(2,1)} %param.3), channel_id=1, source_target_pairs={{0,16},{16,32},{32,48},{1,17},{17,33},{33,49},{2,18},{18,34},{34,5... | collective-permute-start | bytes 184328 | tf_op jit(solution)/shard_map/ppermute | solution.py:12
  4.6 1.2 fusion.28
  5.8 4.8 %collective-permute-start = (bf16[2,1,60,256]{3,1,2,0:T(2,128)(2,1)S(1)}, bf16[2,1,60,256]{3,1,2,0:T(2,128)(2,1)S(1)}, u32[]{:S(2)}, u32[]{:S(2)}) collective-permute-start(bf16[2,1,60,256]{3,1,2,0:T(2,128)(2,1)S(1)} %get-tuple-element.51), channel_id=1, source_target_pairs={{0,1},{1,2},{2,3},{3,4},{4,5},{5,6},{6,7},{7,8},{8,9},{9,10},{10,1... | collective-permute-start | bytes 184328 | tf_op jit(solution)/shard_map/ppermute | solution.py:35
  10.6 1.3 collective-permute-start.1
  11.9 0.9 copy.89
  12.8 0.7 reshape_squeeze.6.grad_ref
  13.6 0.0 collective-permute-done.3
  13.6 1.0 pad_maximum_fusion.6
  14.5 0.3 copy.90
  14.8 1.9 %copy.91 = bf16[16,4,30,16,2]{0,4,3,2,1:T(2,128)(2,1)S(1)} copy(bf16[16,4,30,16,2]{2,4,0,3,1:T(2,128)(2,1)S(1)} %bitcast.111) | data formatting | bytes 245760 | tf_op jit(solution)/shard_map/transpose | solution.py:208
  16.8 1.0 copy.92.lat_ref
  17.8 57.9 %shard_map.50 = (bf16[16,120,512]{2,1,0:T(8,128)(2,1)}, bf16[16,30,128]{2,1,0:T(8,128)(2,1)}) custom-call(bf16[120,512]{1,0:T(8,128)(2,1)} %reshape_squeeze.6.grad_ref, bf16[16,30,128]{2,1,0:T(8,128)(2,1)} %copy.92.lat_ref), custom_call_target="tpu_custom_call" | custom-call | tf_op jit(solution)/shard_map/pallas_call | solution.py:155
  75.8 2.2 %copy.93 = f32[16,120,512]{2,0,1:T(8,128)S(1)} copy(bf16[16,120,512]{2,1,0:T(8,128)(2,1)} %get-tuple-element.4) | data formatting | bytes 5898240 | tf_op jit(solution)/shard_map/convert_element_type | solution.py:217
  78.0 0.6 fusion.24
  78.6 0.8 fusion.25
  79.4 2.1 %copy_bitcast_fusion = (f32[15,2,30,512]{3,2,0,1:T(8,128)S(1)}, f32[15,2,30,512]{3,2,0,1:T(8,128)S(1)}) fusion(f32[15,2,1,30,512]{4,0,3,2,1:T(8,128)S(1)} %get-tuple-element.20, f32[15,2,1,30,512]{4,0,3,2,1:T(8,128)S(1)} %get-tuple-element.19), kind=kLoop, calls=%fused_computation.20 | loop fusion | bytes 7372800 | tf_op jit(solution)/shard_map/slice | solution.py:224
  81.5 1.3 fusion.8
  82.9 2.2 %copy_add_fusion = f32[16,2,1,30,512]{4,3,0,1,2:T(8,128)S(1)} fusion(f32[16,2,1,30,512]{4,0,3,2,1:T(8,128)S(1)} %get-tuple-element.22, f32[16,2,1,30,512]{4,0,3,2,1:T(8,128)S(1)} %get-tuple-element.21), kind=kLoop, calls=%fused_computation.19 | loop fusion | flops 491520 | bytes 5898240 | tf_op jit(solution)/shard_map/add | solution.py:223
  85.0 1.3 fusion.9
  86.3 1.4 %pad_maximum_fusion.1 = f32[16,2,3,30,512]{4,3,0,1,2:T(8,128)S(1)} fusion(f32[16,2,1,30,512]{4,3,0,1,2:T(8,128)S(1)} %fusion.8, f32[16,2,1,30,512]{4,3,0,1,2:T(8,128)S(1)} %copy_add_fusion, f32[16,2,1,30,512]{4,3,0,1,2:T(8,128)S(1)} %fusion.9), kind=kLoop, calls=%fused_computation.9 | loop fusion | flops 2949120 | bytes 11796480 | tf_op jit(solution)/shard_map/stack | solution.py:220
  87.8 0.0 copy-start
  87.8 0.0 copy-start.2
  87.8 4.1 %fusion.23 = (f32[16,2,3,29,256]{4,3,0,1,2:T(8,128)}, f32[16,2,3,29,256]{4,3,0,1,2:T(8,128)}) fusion(f32[16,2,3,30,512]{4,3,0,1,2:T(8,128)S(1)} %pad_maximum_fusion.1), kind=kLoop, calls=%fused_computation.84 | loop fusion | bytes 11403264 | tf_op jit(solution)/shard_map/slice | solution.py:232
  91.8 0.5 copy-done
  92.4 0.0 copy-start.1
  92.4 0.0 copy-done.2
  92.4 0.4 reshape.326
  92.7 0.1 fusion.26
  92.8 0.5 copy.115
  93.3 0.3 copy.116
  93.6 0.3 copy.117
  93.9 0.0 collective-permute-done
  93.9 0.0 collective-permute-done.1
  94.0 0.0 copy-done.1
  94.0 0.4 pad_maximum_fusion.3
  94.4 1.3 collective-permute-start.2
  95.7 6.2 %add_bitcast_fusion.2 = (f32[1,16,2,3,30,1,256]{6,4,1,2,5,3,0:T(8,128)S(1)}, f32[1,16,2,3,30,1,256]{6,4,1,2,5,3,0:T(8,128)S(1)}, f32[1,16,2,3,30,1,256]{6,4,1,2,5,3,0:T(8,128)S(1)}) fusion(f32[16,2,3,29,256]{4,3,0,1,2:T(8,128)} %get-tuple-element.17, f32[16,2,3,30,512]{4,3,0,1,2:T(8,128)} %copy-done, f32[16,2,3,29,256]{4,3,0,1,2:T(8,128)} %get-tuple-element.18), kind=kLoop, calls=%fused_computation.14 | loop fusion | flops 2211840 | bytes 20447232 | tf_op jit(solution)/shard_map/stack | solution.py:230
  101.9 2.3 %fusion.1 = (bf16[1,16,2,3,30,3,256]{6,4,1,2,5,3,0:T(8,128)(2,1)S(1)}, bf16[1,16,2,3,30,3,256]{6,4,1,2,5,3,0:T(8,128)(2,1)S(1)}) fusion(f32[1,16,2,3,30,1,256]{6,4,1,2,5,3,0:T(8,128)S(1)} %get-tuple-element.15, f32[1,16,2,3,30,1,256]{6,4,1,2,5,3,0:T(8,128)S(1)} %get-tuple-element.16, f32[1,16,2,3,30,1,256]{6,4,1,2,5,3,0:T(8,128)S(1)} %get-tuple-element.14), kind=kLoop, calls=%fused_computation.2 | loop fusion | flops 17694720 | bytes 17694720 | tf_op jit(solution)/shard_map/convert.1
  104.2 1.7 %fusion.10 = f32[32,3,3,3,2,256]{5,0,1,3,2,4:T(8,128)S(1)} fusion(bf16[1,16,2,3,30,3,256]{6,4,1,2,5,3,0:T(8,128)(2,1)S(1)} %get-tuple-element.13, bf16[1,16,2,3,30,3,256]{6,4,1,2,5,3,0:T(8,128)(2,1)S(1)} %get-tuple-element.12, bf16[1,16,2,30,32]{3,4,1,2,0:T(8,128)(2,1)S(1)} %bitcast.140, bf16[1,16,2,30,32]{3,4,1,2,0:T(8,128)(2,1)S(1)} %bitcast.139, ...), kind=kOutput, calls=%fused_computation.22 | convolution fusion | flops 867594240 | bytes 10801152 | tf_op jit(solution)/shard_map/arfsc,xrfisjo->caijxo/dot_general | solution.py:241
  106.0 0.1 fusion.17
  106.1 0.6 copy.103
  106.7 1.4 mul.31.term_ref
  108.1 20.8 %shard_map.51 = f32[108,128]{1,0:T(8,128)} custom-call(f32[16,108,128]{2,1,0:T(8,128)} %mul.31.term_ref), custom_call_target="tpu_custom_call" | custom-call | tf_op jit(solution)/shard_map/pallas_call | solution.py:90
  128.9 0.8 reshape.327
  129.7 0.7 copy.105
  130.4 0.5 pad_maximum_fusion.4
  130.9 0.0 collective-permute-done.2
  130.9 0.5 pad_maximum_fusion.2
  131.4 0.2 pad_slice_fusion.17
  131.6 0.7 pad_slice_fusion
  132.3 0.7 pad_slice_fusion.1
  133.1 0.3 fusion.27
  134.0 5.0 %fusion.14 = bf16[2,30,512]{2,1,0:T(8,128)(2,1)S(1)} fusion(bf16[27,512,256,1,1,1]{2,1,0,5,4,3:T(8,128)(2,1)} %bitcast.142, bf16[2,1,2,30,2,27,256]{6,3,5,4,2,0,1:T(8,128)(2,1)S(1)} %copy_dynamic-update-slice_fusion), kind=kOutput, calls=%fused_computation.24 | convolution fusion | flops 1698785280 | bytes 10457088 | tf_op jit(solution)/shard_map/dot_general | solution.py:193
  139.1 0.7 copy.104
  (27 shorter events, 0.5 us)
Async XLA Ops:
  0.6 12.9 %collective-permute-start.3 = (bf16[1,2,1,30,512]{4,1,3,2,0:T(2,128)(2,1)}, bf16[1,2,1,30,512]{4,1,3,2,0:T(2,128)(2,1)S(1)}, u32[]{:S(2)}, u32[]{:S(2)}) collective-permute-start(bf16[1,2,1,30,512]{4,1,3,2,0:T(2,128)(2,1)} %param.3), channel_id=1, source_target_pairs={{0,16},{16,32},{32,48},{1,17},{17,33},{33,49},{2,18},{18,34},{34,5... | collective-permute-start | bytes 184328 | tf_op jit(solution)/shard_map/ppermute | solution.py:12
  5.8 88.2 %collective-permute-start = (bf16[2,1,60,256]{3,1,2,0:T(2,128)(2,1)S(1)}, bf16[2,1,60,256]{3,1,2,0:T(2,128)(2,1)S(1)}, u32[]{:S(2)}, u32[]{:S(2)}) collective-permute-start(bf16[2,1,60,256]{3,1,2,0:T(2,128)(2,1)S(1)} %get-tuple-element.51), channel_id=1, source_target_pairs={{0,1},{1,2},{2,3},{3,4},{4,5},{5,6},{6,7},{7,8},{8,9},{9,10},{10,1... | collective-permute-start | bytes 184328 | tf_op jit(solution)/shard_map/ppermute | solution.py:35
  10.6 83.3 %collective-permute-start.1 = (bf16[2,1,60,256]{3,1,2,0:T(2,128)(2,1)S(1)}, bf16[2,1,60,256]{3,1,2,0:T(2,128)(2,1)S(1)}, u32[]{:S(2)}, u32[]{:S(2)}) collective-permute-start(bf16[2,1,60,256]{3,1,2,0:T(2,128)(2,1)S(1)} %get-tuple-element.52), channel_id=1, source_target_pairs={{1,0},{2,1},{3,2},{4,3},{5,4},{6,5},{7,6},{8,7},{9,8},{10,9},{11,1... | collective-permute-start | bytes 184328 | tf_op jit(solution)/shard_map/ppermute | solution.py:38
  87.8 4.6 %copy-start = (f32[16,2,3,30,512]{4,3,0,1,2:T(8,128)}, f32[16,2,3,30,512]{4,3,0,1,2:T(8,128)S(1)}, u32[]{:S(2)}) copy-start(f32[16,2,3,30,512]{4,3,0,1,2:T(8,128)S(1)} %pad_maximum_fusion.1) | copy-start | bytes 17694724
  87.8 4.6 %copy-start.2 = (bf16[16,30,128]{2,1,0:T(8,128)(2,1)S(1)}, bf16[16,30,128]{2,1,0:T(8,128)(2,1)}, u32[]{:S(2)}) copy-start(bf16[16,30,128]{2,1,0:T(8,128)(2,1)} %get-tuple-element.5) | copy-start | bytes 368644
  92.4 1.6 %copy-start.1 = (bf16[1,2,2,60,256]{4,2,3,1,0:T(2,128)(2,1)S(1)}, bf16[1,2,2,60,256]{4,2,3,1,0:T(2,128)(2,1)}, u32[]{:S(2)}) copy-start(bf16[1,2,2,60,256]{4,2,3,1,0:T(2,128)(2,1)} %param.4) | copy-start | bytes 368644
  94.4 36.5 %collective-permute-start.2 = (bf16[2,4,60,256]{3,1,2,0:T(4,128)(2,1)S(1)}, bf16[2,4,60,256]{3,1,2,0:T(4,128)(2,1)S(1)}, u32[]{:S(2)}, u32[]{:S(2)}) collective-permute-start(bf16[2,4,60,256]{3,1,2,0:T(4,128)(2,1)S(1)} %pad_maximum_fusion.3), channel_id=1, source_target_pairs={{16,0},{32,16},{48,32},{17,1},{33,17},{49,33},{18,2},{34,18},{50,3... | collective-permute-start | bytes 737288 | tf_op jit(solution)/shard_map/ppermute | solution.py:12

commit v4 on v3

--- a/solution.py
+++ b/solution.py
@@ -39,15 +39,26 @@
     return jnp.concatenate([low, block, high], axis=dim)
 
 
+def rows_group():
+    def device(k):
+        return (lax.axis_index("dp"), lax.axis_index("tm"), k)
+
+    return lax.axis_size("rows"), lax.axis_index("rows"), device
+
+
+def blocks_group():
+    tm_size = lax.axis_size("tm")
+
+    def device(k):
+        return (k // tm_size, k % tm_size, lax.axis_index("rows"))
+
+    me = lax.axis_index("dp") * tm_size + lax.axis_index("tm")
+    return lax.axis_size("dp") * tm_size, me, device
+
+
 def scatter_sum_kernel(term_ref, out_ref, slots, send_sem, recv_sem):
-    tm_size = lax.axis_size("tm")
-    count = lax.axis_size("dp") * tm_size
-    row = lax.axis_index("rows")
-    me = lax.axis_index("dp") * tm_size + lax.axis_index("tm")
+    count, me, device = rows_group()
     mesh_id = pl.DeviceIdType.MESH
-
-    def device(k):
-        return (k // tm_size, k % tm_size, row)
 
     barrier = pltpu.get_barrier_semaphore()
     for d in range(1, count):
@@ -101,13 +112,9 @@
     )(term)
 
 
-def row_exchange_kernel(grad_ref, lat_ref, grad_buf, lat_buf, send_sem, recv_sem):
-    count = lax.axis_size("rows")
-    me = lax.axis_index("rows")
+def block_exchange_kernel(grad_ref, lat_ref, grad_buf, lat_buf, send_sem, recv_sem):
+    count, me, device = blocks_group()
     mesh_id = pl.DeviceIdType.MESH
-
-    def device(k):
-        return (lax.axis_index("dp"), lax.axis_index("tm"), k)
 
     barrier = pltpu.get_barrier_semaphore()
     for d in range(1, count):
@@ -150,10 +157,10 @@
         copy.wait_send()
 
 
-def row_exchange(grad_send, lat_send):
+def block_exchange(grad_send, lat_send):
     count = lat_send.shape[0]
     return pl.pallas_call(
-        row_exchange_kernel,
+        block_exchange_kernel,
         out_shape=(
             jax.ShapeDtypeStruct((count,) + grad_send.shape, grad_send.dtype),
             jax.ShapeDtypeStruct(lat_send.shape, lat_send.dtype),
@@ -200,32 +207,27 @@
     grad_latents = pooled.astype(jnp.bfloat16)[None]
 
     groups = lax.axis_size("dp") * lax.axis_size("tm")
+    clips = lax.axis_size("dp")
     share = channels // devices
-    earlier = shift_from(latents, "tm", 1)
-    with_earlier = jnp.concatenate([earlier, latents], axis=1)[0, :, 0]
-    lead = with_earlier.shape[:2]
-    regrouped = with_earlier.reshape(lead + (groups, slab_count, share))
-    regrouped = jnp.transpose(regrouped, (3, 0, 1, 2, 4))
-    lat_send = regrouped.reshape(slab_count, -1, 128)
+    group_channels = channels // groups
+    lat_rows = with_halo(latents[0], "rows", 1, 1)
+    lat_send = lat_rows.reshape(frames, 3, width // 2, groups, group_channels)
+    lat_send = jnp.transpose(lat_send, (3, 0, 1, 2, 4)).reshape(groups, -1, 128)
     grad_send = grad_out[0].reshape(frames * height * (width // 2), 2 * outputs)
-    grad_buf, lat_buf = row_exchange(grad_send, lat_send)
-    group_channels = groups * share
-    owned = lat_buf.reshape(slab_count, lead[0], width // 2, group_channels)
-    taps_a = jnp.stack([owned[:, a : a + frames] for a in range(3)], axis=0)
-
-    whole = grad_buf.reshape(slab_count, frames, height, width // 2, 2 * outputs)
+    grad_buf, lat_buf = block_exchange(grad_send, lat_send)
+    all_frames = groups // clips * frames
+    owned = lat_buf.reshape(clips, all_frames, 3, width // 2, group_channels)
+    owned = jnp.pad(owned, ((0, 0), (2, 0), (0, 0), (0, 0), (0, 0)))
+    taps = []
+    for a in range(3):
+        for i in range(3):
+            per_row = [owned[:, a : a + all_frames, (r - 1 + i) // 2 + 1] for r in range(height)]
+            taps.append(jnp.stack(per_row, axis=2))
+    taps = jnp.stack(taps, axis=0)
+
+    whole = grad_buf.reshape(clips, all_frames, height, width // 2, 2 * outputs)
     whole = whole.astype(jnp.float32)
-    top_row, bottom_row = whole[:, :, 0], whole[:, :, 1]
-    zero = jnp.zeros_like(top_row[:1])
-    rows_pooled = jnp.stack(
-        [
-            bottom_row + jnp.concatenate([top_row[1:], zero], axis=0),
-            top_row + bottom_row,
-            top_row + jnp.concatenate([zero, bottom_row[:-1]], axis=0),
-        ],
-        axis=2,
-    )
-    left, right = rows_pooled[..., :outputs], rows_pooled[..., outputs:]
+    left, right = whole[..., :outputs], whole[..., outputs:]
     zero = jnp.zeros_like(left[:, :, :, :1])
     pooled_grad = jnp.stack(
         [
@@ -239,11 +241,11 @@
     top = scaled - (scaled - pooled_grad)
     both = jnp.stack([top, pooled_grad - top], axis=0).astype(jnp.bfloat16)
     term = jnp.einsum(
-        "arfsc,xrfisjo->caijxo", taps_a, both, preferred_element_type=jnp.float32
+        "kbflsc,xbflsjo->ckjxo", taps, both, preferred_element_type=jnp.float32
     )
     term = (term[..., 0, :] + term[..., 1, :]) * factor
     share_size = share * 27 * outputs
-    term = term.reshape(groups, share_size // 128, 128)
+    term = term.reshape(slab_count, share_size // 128, 128)
     weight_grad = scatter_sum(term).reshape(share, 3, 3, 3, outputs)
     return (grad_latents, weight_grad)
 

time: 140 us -> 129 us (0.921); the launches traced: 140 us -> 127 us
  Pallas kernels: 78.7 us -> 66.9 us
  other arithmetic: 17.3 us -> 8.03 us
  starting transfers between devices: 11.4 us -> 16.1 us
  local copies, waits for them, and re-layouts: 24.5 us -> 27.3 us
    pallas_call x1, Pallas kernels: 57.9 us -> 34.5 us  [block_exchange(): pl.pallas_call(block_exchange_kernel, out_shape=(jax.ShapeDtypeStruct((co...]
    pallas_call x1, Pallas kernels: 20.8 us -> 32.4 us  [scatter_sum(): pl.pallas_call(scatter_sum_kernel, out_shape=jax.ShapeDtypeStruct((rows,...]
    ppermute x1 -> x2, starting transfers between devices: 4.83 us -> 12 us  [with_halo(): lax.ppermute(lax.slice_in_dim(block, block.shape[dim] - width, None, axis...]
    another operation x4 -> x1, other arithmetic: 6.37 us -> 1.52 us  [the longest x3 4.06 us: body(): jnp.stack([bottom_row + jnp.concatenate([top_row[1:], zero], axis=0), top...]
    another operation x1, other arithmetic: 6.19 us -> 1.37 us  [body(): jnp.stack([right + jnp.concatenate([left[:, :, :, 1:], zero], axis=3), le...]
    unnamed x38 -> x48, local copies, waits for them, and re-layouts: 4.31 us -> 8.15 us
    ppermute x2 -> x1, starting transfers between devices: 5.24 us -> 1.46 us  [shift_from(): return lax.ppermute(shard, axis, pairs)]
    slice x4 -> x1, local copies, waits for them, and re-layouts: 3.66 us -> 0.99 us  [body(): owned[:, a:a + all_frames, (r - 1 + i) // 2 + 1]]
  transfers between devices with their start and end apart: 4 -> 5, of which waited for: 0 -> 0; matrix products, arithmetic and copies ran while one was open for 28% -> 25% of each run, Pallas kernels for 56% -> 53%
where the time goes in v4:
time: 129 us; the launch traced here: 127 us
  Pallas kernels  66.9 us (52%)
  local copies, waits for them, and re-layouts  27.3 us (21%)
  starting transfers between devices  16.1 us (12%)
  other arithmetic  8.03 us (6%)
  matrix products  7.23 us (6%)
    pallas_call x1, Pallas kernels, block_exchange(): pl.pallas_call(block_exchange_kernel, out_shape=(jax.ShapeDtypeStruct((co...  34.5 us
    pallas_call x1, Pallas kernels, scatter_sum(): pl.pallas_call(scatter_sum_kernel, out_shape=jax.ShapeDtypeStruct((rows,...  32.4 us
    ppermute x2, starting transfers between devices, with_halo(): lax.ppermute(lax.slice_in_dim(block, block.shape[dim] - width, None, axis...  12 us
    unnamed x48, local copies, waits for them, and re-layouts  8.15 us
    dot_general x1, matrix products, body(): lax.dot_general(patches, kernel.reshape(27, channels, outputs), (((1, 2),...  5.04 us
    slice x1, local copies, waits for them, and re-layouts, body(): left[:, :, :, 1:]  2.78 us
    unnamed x3, other arithmetic  2.62 us
    ppermute x2, starting transfers between devices, with_halo(): lax.ppermute(lax.slice_in_dim(block, 0, width, axis=dim), axis, backward)  2.58 us
  transfers between devices with their start and end apart: 5, of which 0 were waited for; matrix products, arithmetic and copies ran while one was open for 25% of the time, Pallas kernels for 53%

profile of v4, /device:TPU:1, one launch (start us, length us, event | category | flops | bytes accessed | tf_op | source)
XLA Modules:
  0.0 126.8 jit_solution(1383955928103434708)
XLA Ops:
  0.6 1.3 %collective-permute-start.4 = (bf16[2,1,30,512]{3,0,2,1:T(2,128)(2,1)}, bf16[2,1,30,512]{3,0,2,1:T(2,128)(2,1)S(1)}, u32[]{:S(2)}, u32[]{:S(2)}) collective-permute-start(bf16[2,1,30,512]{3,0,2,1:T(2,128)(2,1)} %bitcast.154), channel_id=1, source_target_pairs={{1,0},{2,1},{3,2},{4,3},{5,4},{6,5},{7,6},{8,7},{9,8},{10,9},{11,1... | collective-permute-start | bytes 184328 | tf_op jit(solution)/shard_map/ppermute | solution.py:38
  1.9 6.3 %collective-permute-start.3 = (bf16[2,1,30,512]{3,0,2,1:T(2,128)(2,1)}, bf16[2,1,30,512]{3,0,2,1:T(2,128)(2,1)S(1)}, u32[]{:S(2)}, u32[]{:S(2)}) collective-permute-start(bf16[2,1,30,512]{3,0,2,1:T(2,128)(2,1)} %bitcast.155), channel_id=1, source_target_pairs={{0,1},{1,2},{2,3},{3,4},{4,5},{5,6},{6,7},{7,8},{8,9},{9,10},{10,1... | collective-permute-start | bytes 184328 | tf_op jit(solution)/shard_map/ppermute | solution.py:35
  8.2 1.8 %fusion.36 = (bf16[2,1,60,256]{3,1,2,0:T(2,128)(2,1)}, bf16[2,1,60,256]{3,1,2,0:T(2,128)(2,1)S(1)}) fusion(bf16[2,2,60,256]{3,1,2,0:T(2,128)(2,1)} %bitcast.122), kind=kLoop, calls=%fused_computation.99 | loop fusion | bytes 245760 | tf_op jit(solution)/shard_map/slice | solution.py:36
  10.0 5.8 %collective-permute-start = (bf16[2,1,60,256]{3,1,2,0:T(2,128)(2,1)}, bf16[2,1,60,256]{3,1,2,0:T(2,128)(2,1)S(1)}, u32[]{:S(2)}, u32[]{:S(2)}) collective-permute-start(bf16[2,1,60,256]{3,1,2,0:T(2,128)(2,1)} %get-tuple-element.47), channel_id=1, source_target_pairs={{0,1},{1,2},{2,3},{3,4},{4,5},{5,6},{6,7},{7,8},{8,9},{9,10},{10,1... | collective-permute-start | bytes 184328 | tf_op jit(solution)/shard_map/ppermute | solution.py:35
  15.8 1.3 %collective-permute-start.1 = (bf16[2,1,60,256]{3,1,2,0:T(2,128)(2,1)S(1)}, bf16[2,1,60,256]{3,1,2,0:T(2,128)(2,1)S(1)}, u32[]{:S(2)}, u32[]{:S(2)}) collective-permute-start(bf16[2,1,60,256]{3,1,2,0:T(2,128)(2,1)S(1)} %get-tuple-element.48), channel_id=1, source_target_pairs={{1,0},{2,1},{3,2},{4,3},{5,4},{6,5},{7,6},{8,7},{9,8},{10,9},{11,1... | collective-permute-start | bytes 184328 | tf_op jit(solution)/shard_map/ppermute | solution.py:38
  17.1 0.9 copy.79
  18.0 1.0 concatenate.61
  19.1 0.7 reshape_squeeze.3.grad_ref
  19.8 0.1 copy.81
  19.9 0.0 collective-permute-done.3
  19.9 0.2 concatenate.60
  20.1 0.1 copy.80
  20.2 0.0 collective-permute-done.4
  20.2 0.2 concatenate.62
  20.4 0.1 copy.82
  20.5 0.2 maximum_bitcast_fusion.4
  20.7 0.0 copy-start.1
  20.7 1.2 reshape.328.lat_ref
  21.9 34.5 %shard_map.50 = (bf16[16,120,512]{2,1,0:T(8,128)(2,1)}, bf16[16,45,128]{2,1,0:T(8,128)(2,1)}) custom-call(bf16[120,512]{1,0:T(8,128)(2,1)} %reshape_squeeze.3.grad_ref, bf16[16,45,128]{2,1,0:T(8,128)(2,1)} %reshape.328.lat_ref), custom_call_target="tpu_custom_call" | custom-call | tf_op jit(solution)/shard_map/pallas_call | solution.py:162
  56.4 1.5 %reshape.329 = bf16[4,8,3,30,32]{4,3,2,1,0:T(8,128)(2,1)S(1)} reshape(bf16[16,45,128]{2,1,0:T(8,128)(2,1)} %get-tuple-element.5) | data formatting | bytes 368640 | tf_op jit(solution)/shard_map/reshape | solution.py:219
  57.9 0.7 copy.83
  58.6 1.0 fusion.34
  59.6 0.9 fusion.20
  60.5 0.0 collective-permute-done
  60.5 0.0 collective-permute-done.1
  60.5 0.0 copy-done.1
  60.5 1.1 pad_maximum_fusion.2
  61.6 1.5 %collective-permute-start.2 = (bf16[2,4,60,256]{3,1,2,0:T(4,128)(2,1)}, bf16[2,4,60,256]{3,1,2,0:T(4,128)(2,1)S(1)}, u32[]{:S(2)}, u32[]{:S(2)}) collective-permute-start(bf16[2,4,60,256]{3,1,2,0:T(4,128)(2,1)} %pad_maximum_fusion.2), channel_id=1, source_target_pairs={{16,0},{32,16},{48,32},{17,1},{33,17},{49,33},{18,2},{34,18},{50,3... | collective-permute-start | bytes 737288 | tf_op jit(solution)/shard_map/ppermute | solution.py:12
  63.1 0.0 copy-done.2
  63.1 2.2 %reshape.331 = f32[4,8,2,30,512]{4,3,2,1,0:T(8,128)} reshape(bf16[16,120,512]{2,1,0:T(8,128)(2,1)S(1)} %copy-done.2) | data formatting | bytes 5898240 | tf_op jit(solution)/shard_map/convert_element_type | solution.py:229
  65.4 2.8 %fusion.33 = (f32[4,8,2,29,256]{4,3,2,1,0:T(8,128)S(1)}, f32[4,8,2,29,256]{4,3,2,1,0:T(8,128)S(1)}) fusion(f32[4,8,2,30,512]{4,3,2,1,0:T(8,128)} %reshape.331), kind=kLoop, calls=%fused_computation.96 | loop fusion | bytes 7602176 | tf_op jit(solution)/shard_map/slice | solution.py:234
  68.1 0.0 copy-start.4
  68.2 0.0 copy-start.3
  68.2 0.0 copy-done.5
  68.2 0.9 fusion.29
  69.0 0.9 fusion.22
  70.0 1.0 fusion.24
  70.9 0.0 copy-done.4
  70.9 0.9 fusion.30
  71.8 0.9 fusion.26
  72.7 0.9 fusion.28
  73.6 0.0 copy-done.3
  73.6 0.9 fusion.31
  74.5 0.9 fusion.27
  75.3 0.0 copy-done
  75.3 1.4 %add_bitcast_fusion.2 = (f32[1,4,8,2,30,1,256]{6,4,3,2,1,5,0:T(8,128)S(1)}, f32[1,4,8,2,30,1,256]{6,4,3,2,1,5,0:T(8,128)S(1)}, f32[1,4,8,2,30,1,256]{6,4,3,2,1,5,0:T(8,128)S(1)}) fusion(f32[4,8,2,29,256]{4,3,2,1,0:T(8,128)S(1)} %get-tuple-element.17, f32[4,8,2,30,512]{4,3,2,1,0:T(8,128)S(1)} %copy-done, f32[4,8,2,29,256]{4,3,2,1,0:T(8,128)S(1)} %get-tuple-element.18), kind=kLoop, calls=%fused_computation.14 | loop fusion | flops 1474560 | bytes 13631488 | tf_op jit(solution)/shard_map/stack | solution.py:232
  76.7 1.5 %fusion.1 = (bf16[1,4,8,2,30,3,256]{6,4,3,2,1,5,0:T(8,128)(2,1)S(1)}, bf16[1,4,8,2,30,3,256]{6,4,3,2,1,5,0:T(8,128)(2,1)S(1)}) fusion(f32[1,4,8,2,30,1,256]{6,4,3,2,1,5,0:T(8,128)S(1)} %get-tuple-element.15, f32[1,4,8,2,30,1,256]{6,4,3,2,1,5,0:T(8,128)S(1)} %get-tuple-element.16, f32[1,4,8,2,30,1,256]{6,4,3,2,1,5,0:T(8,128)S(1)} %get-tuple-element.14), kind=kLoop, calls=%fused_computation.2 | loop fusion | flops 11796480 | bytes 11796480 | tf_op jit(solution)/shard_map/convert.1
  78.3 0.8 copy-done.6
  79.1 2.2 %fusion.9 = f32[32,9,3,2,256]{4,0,1,2,3:T(8,128)S(1)} fusion(bf16[9,4,8,2,30,32]{4,5,3,2,1,0:T(8,128)(2,1)S(1)} %copy-done.6, bf16[1,4,8,2,30,3,256]{6,4,3,2,1,5,0:T(8,128)(2,1)S(1)} %get-tuple-element.13, bf16[1,4,8,2,30,3,256]{6,4,3,2,1,5,0:T(8,128)(2,1)S(1)} %get-tuple-element.12), kind=kOutput, calls=%fused_computation.15 | convolution fusion | flops 1710489600 | bytes 8773632 | tf_op jit(solution)/shard_map/kbflsc,xbflsjo->ckjxo/dot_general | solution.py:243
  81.3 0.2 fusion.18
  81.4 0.6 copy.87
  82.0 1.4 %mul.31.term_ref = f32[16,108,128]{2,1,0:T(8,128)} reshape(f32[32,9,3,1,256]{4,2,1,0,3:T(4,128)S(1)} %copy.87) | data formatting | bytes 1769472 | tf_op jit(solution)/shard_map/mul | solution.py:246
  83.4 32.4 %shard_map.51 = f32[108,128]{1,0:T(8,128)} custom-call(f32[16,108,128]{2,1,0:T(8,128)} %mul.31.term_ref), custom_call_target="tpu_custom_call" | custom-call | tf_op jit(solution)/shard_map/pallas_call | solution.py:101
  115.9 0.8 reshape.330
  116.7 0.7 copy.89
  117.4 0.5 pad_maximum_fusion.3
  117.9 0.0 collective-permute-done.2
  117.9 0.5 pad_maximum_fusion.1
  118.5 0.2 pad_slice_fusion.23
  118.6 0.7 pad_slice_fusion.6
  119.3 0.7 pad_slice_fusion.7
  120.1 0.3 fusion.35
  121.0 5.0 %fusion.15 = bf16[2,30,512]{2,1,0:T(8,128)(2,1)S(1)} fusion(bf16[27,512,256,1,1,1]{2,1,0,5,4,3:T(8,128)(2,1)} %bitcast.156, bf16[2,1,2,30,2,27,256]{6,3,5,4,2,0,1:T(8,128)(2,1)S(1)} %copy_dynamic-update-slice_fusion), kind=kOutput, calls=%fused_computation.17 | convolution fusion | flops 1698785280 | bytes 10457088 | tf_op jit(solution)/shard_map/dot_general | solution.py:200
  126.1 0.7 copy.88
  (31 shorter events, 0.5 us)
Async XLA Ops:
  0.6 19.6 %collective-permute-start.4 = (bf16[2,1,30,512]{3,0,2,1:T(2,128)(2,1)}, bf16[2,1,30,512]{3,0,2,1:T(2,128)(2,1)S(1)}, u32[]{:S(2)}, u32[]{:S(2)}) collective-permute-start(bf16[2,1,30,512]{3,0,2,1:T(2,128)(2,1)} %bitcast.154), channel_id=1, source_target_pairs={{1,0},{2,1},{3,2},{4,3},{5,4},{6,5},{7,6},{8,7},{9,8},{10,9},{11,1... | collective-permute-start | bytes 184328 | tf_op jit(solution)/shard_map/ppermute | solution.py:38
  1.9 18.0 %collective-permute-start.3 = (bf16[2,1,30,512]{3,0,2,1:T(2,128)(2,1)}, bf16[2,1,30,512]{3,0,2,1:T(2,128)(2,1)S(1)}, u32[]{:S(2)}, u32[]{:S(2)}) collective-permute-start(bf16[2,1,30,512]{3,0,2,1:T(2,128)(2,1)} %bitcast.155), channel_id=1, source_target_pairs={{0,1},{1,2},{2,3},{3,4},{4,5},{5,6},{6,7},{7,8},{8,9},{9,10},{10,1... | collective-permute-start | bytes 184328 | tf_op jit(solution)/shard_map/ppermute | solution.py:35
  10.0 50.4 %collective-permute-start = (bf16[2,1,60,256]{3,1,2,0:T(2,128)(2,1)}, bf16[2,1,60,256]{3,1,2,0:T(2,128)(2,1)S(1)}, u32[]{:S(2)}, u32[]{:S(2)}) collective-permute-start(bf16[2,1,60,256]{3,1,2,0:T(2,128)(2,1)} %get-tuple-element.47), channel_id=1, source_target_pairs={{0,1},{1,2},{2,3},{3,4},{4,5},{5,6},{6,7},{7,8},{8,9},{9,10},{10,1... | collective-permute-start | bytes 184328 | tf_op jit(solution)/shard_map/ppermute | solution.py:35
  15.8 44.7 %collective-permute-start.1 = (bf16[2,1,60,256]{3,1,2,0:T(2,128)(2,1)S(1)}, bf16[2,1,60,256]{3,1,2,0:T(2,128)(2,1)S(1)}, u32[]{:S(2)}, u32[]{:S(2)}) collective-permute-start(bf16[2,1,60,256]{3,1,2,0:T(2,128)(2,1)S(1)} %get-tuple-element.48), channel_id=1, source_target_pairs={{1,0},{2,1},{3,2},{4,3},{5,4},{6,5},{7,6},{8,7},{9,8},{10,9},{11,1... | collective-permute-start | bytes 184328 | tf_op jit(solution)/shard_map/ppermute | solution.py:38
  20.7 39.8 %copy-start.1 = (bf16[1,2,2,60,256]{4,2,3,1,0:T(2,128)(2,1)S(1)}, bf16[1,2,2,60,256]{4,2,3,1,0:T(2,128)(2,1)}, u32[]{:S(2)}) copy-start(bf16[1,2,2,60,256]{4,2,3,1,0:T(2,128)(2,1)} %param.4) | copy-start | bytes 368644
  58.6 4.5 %copy-start.2 = (bf16[16,120,512]{2,1,0:T(8,128)(2,1)S(1)}, bf16[16,120,512]{2,1,0:T(8,128)(2,1)}, u32[]{:S(2)}) copy-start(bf16[16,120,512]{2,1,0:T(8,128)(2,1)} %get-tuple-element.4) | copy-start | bytes 5898244
  61.6 56.3 %collective-permute-start.2 = (bf16[2,4,60,256]{3,1,2,0:T(4,128)(2,1)}, bf16[2,4,60,256]{3,1,2,0:T(4,128)(2,1)S(1)}, u32[]{:S(2)}, u32[]{:S(2)}) collective-permute-start(bf16[2,4,60,256]{3,1,2,0:T(4,128)(2,1)} %pad_maximum_fusion.2), channel_id=1, source_target_pairs={{16,0},{32,16},{48,32},{17,1},{33,17},{49,33},{18,2},{34,18},{50,3... | collective-permute-start | bytes 737288 | tf_op jit(solution)/shard_map/ppermute | solution.py:12
  65.4 2.8 %copy-start.5 = (bf16[4,8,1,30,32]{3,4,2,1,0:T(8,128)(2,1)S(1)}, bf16[4,8,1,30,32]{3,4,2,1,0:T(8,128)(2,1)}, u32[]{:S(2)}) copy-start(bf16[4,8,1,30,32]{3,4,2,1,0:T(8,128)(2,1)} %get-tuple-element.20) | copy-start | bytes 184324
  68.1 2.8 %copy-start.4 = (bf16[4,8,1,30,32]{3,4,2,1,0:T(8,128)(2,1)S(1)}, bf16[4,8,1,30,32]{3,4,2,1,0:T(8,128)(2,1)}, u32[]{:S(2)}) copy-start(bf16[4,8,1,30,32]{3,4,2,1,0:T(8,128)(2,1)} %get-tuple-element.21) | copy-start | bytes 184324
  68.2 5.5 %copy-start.3 = (bf16[4,8,1,30,32]{3,4,2,1,0:T(8,128)(2,1)S(1)}, bf16[4,8,1,30,32]{3,4,2,1,0:T(8,128)(2,1)}, u32[]{:S(2)}) copy-start(bf16[4,8,1,30,32]{3,4,2,1,0:T(8,128)(2,1)} %get-tuple-element.19) | copy-start | bytes 184324
  69.0 6.3 %copy-start = (f32[4,8,2,30,512]{4,3,2,1,0:T(8,128)S(1)}, f32[4,8,2,30,512]{4,3,2,1,0:T(8,128)}, u32[]{:S(2)}) copy-start(f32[4,8,2,30,512]{4,3,2,1,0:T(8,128)} %reshape.331) | copy-start | bytes 11796484
  76.7 2.3 %copy-start.6 = (bf16[9,4,8,2,30,32]{4,5,3,2,1,0:T(8,128)(2,1)S(1)}, bf16[9,4,8,2,30,32]{4,5,3,2,1,0:T(8,128)(2,1)}, u32[]{:S(2)}) copy-start(bf16[9,4,8,2,30,32]{4,5,3,2,1,0:T(8,128)(2,1)} %fusion.27) | copy-start | bytes 3317764

commit v5 on v4

--- a/solution.py
+++ b/solution.py
@@ -56,41 +56,60 @@
     return lax.axis_size("dp") * tm_size, me, device
 
 
-def scatter_sum_kernel(term_ref, out_ref, slots, send_sem, recv_sem):
+def scatter_sum_kernel(term_ref, out_ref, half, partial, whole, sems):
     count, me, device = rows_group()
+    ring = count // 2
+    z, parity = me // 2, me % 2
+    partner = me + 1 - 2 * parity
     mesh_id = pl.DeviceIdType.MESH
+    send_half, recv_half, send_ring, recv_ring = sems
 
     barrier = pltpu.get_barrier_semaphore()
-    for d in range(1, count):
-        pl.semaphore_signal(barrier, inc=1, device_id=device((me + d) % count), device_id_type=mesh_id)
-    pl.semaphore_wait(barrier, count - 1)
+    pl.semaphore_signal(barrier, inc=1, device_id=device(partner), device_id_type=mesh_id)
+    for d in range(1, ring):
+        peer = ((z + d) % ring) * 2 + parity
+        pl.semaphore_signal(barrier, inc=1, device_id=device(peer), device_id_type=mesh_id)
+    pl.semaphore_wait(barrier, ring)
+
+    def half_copy(m):
+        return pltpu.make_async_remote_copy(
+            src_ref=term_ref.at[2 * m + 1 - parity],
+            dst_ref=half.at[m],
+            send_sem=send_half.at[m],
+            recv_sem=recv_half.at[m],
+            device_id=device(partner),
+            device_id_type=mesh_id,
+        )
 
     copies = []
-    for d in range(1, count):
-        target = (me + d) % count
-        copy = pltpu.make_async_remote_copy(
-            src_ref=term_ref.at[target],
-            dst_ref=slots.at[me],
-            send_sem=send_sem.at[d - 1],
-            recv_sem=recv_sem.at[me],
-            device_id=device(target),
-            device_id_type=mesh_id,
-        )
+    for m in range(ring):
+        copy = half_copy(m)
         copy.start()
         copies.append(copy)
-    total = term_ref[me]
-    for d in range(1, count):
-        source = (me + count - d) % count
-        incoming = pltpu.make_async_remote_copy(
-            src_ref=term_ref.at[source],
-            dst_ref=slots.at[source],
-            send_sem=send_sem.at[d - 1],
-            recv_sem=recv_sem.at[source],
-            device_id=device(source),
-            device_id_type=mesh_id,
-        )
-        incoming.wait_recv()
-        total = total + slots[source]
+    for m in range(ring):
+        half_copy(m).wait_recv()
+        partial[m] = term_ref[2 * m + parity] + half[m]
+
+    def ring_copy(d, peer_z, slot):
+        return pltpu.make_async_remote_copy(
+            src_ref=partial.at[peer_z],
+            dst_ref=whole.at[slot],
+            send_sem=send_ring.at[d - 1],
+            recv_sem=recv_ring.at[slot],
+            device_id=device(peer_z * 2 + parity),
+            device_id_type=mesh_id,
+        )
+
+    for d in range(1, ring):
+        target = (z + d) % ring
+        copy = ring_copy(d, target, z)
+        copy.start()
+        copies.append(copy)
+    total = partial[z]
+    for d in range(1, ring):
+        source = (z + ring - d) % ring
+        ring_copy(d, source, source).wait_recv()
+        total = total + whole[source]
     out_ref[...] = total
     for copy in copies:
         copy.wait_send()
@@ -98,15 +117,22 @@
 
 def scatter_sum(term):
     count, rows, lanes = term.shape
+    ring = count // 2
     return pl.pallas_call(
         scatter_sum_kernel,
         out_shape=jax.ShapeDtypeStruct((rows, lanes), term.dtype),
         in_specs=[pl.BlockSpec(memory_space=pltpu.VMEM)],
         out_specs=pl.BlockSpec(memory_space=pltpu.VMEM),
         scratch_shapes=[
-            pltpu.VMEM((count, rows, lanes), term.dtype),
-            pltpu.SemaphoreType.DMA((count - 1,)),
-            pltpu.SemaphoreType.DMA((count,)),
+            pltpu.VMEM((ring, rows, lanes), term.dtype),
+            pltpu.VMEM((ring, rows, lanes), term.dtype),
+            pltpu.VMEM((ring, rows, lanes), term.dtype),
+            (
+                pltpu.SemaphoreType.DMA((ring,)),
+                pltpu.SemaphoreType.DMA((ring,)),
+                pltpu.SemaphoreType.DMA((ring - 1,)),
+                pltpu.SemaphoreType.DMA((ring,)),
+            ),
         ],
         compiler_params=pltpu.CompilerParams(collective_id=0, has_side_effects=True),
     )(term)

time: 129 us -> 129 us (level)
  no operation moved by 1% of the time
where the time goes in v5:
time: 129 us; the launch traced here: 127 us
  Pallas kernels  67.2 us (52%)
  local copies, waits for them, and re-layouts  27.3 us (21%)
  starting transfers between devices  16.1 us (12%)
  other arithmetic  8.03 us (6%)
  matrix products  7.23 us (6%)
    pallas_call x1, Pallas kernels, block_exchange(): pl.pallas_call(block_exchange_kernel, out_shape=(jax.ShapeDtypeStruct((co...  34.5 us
    pallas_call x1, Pallas kernels, scatter_sum(): pl.pallas_call(scatter_sum_kernel, out_shape=jax.ShapeDtypeStruct((rows,...  32.7 us
    ppermute x2, starting transfers between devices, with_halo(): lax.ppermute(lax.slice_in_dim(block, block.shape[dim] - width, None, axis...  12 us
    unnamed x48, local copies, waits for them, and re-layouts  8.15 us
    dot_general x1, matrix products, body(): lax.dot_general(patches, kernel.reshape(27, channels, outputs), (((1, 2),...  5.04 us
    slice x1, local copies, waits for them, and re-layouts, body(): left[:, :, :, 1:]  2.78 us
    unnamed x3, other arithmetic  2.62 us
    ppermute x2, starting transfers between devices, with_halo(): lax.ppermute(lax.slice_in_dim(block, 0, width, axis=dim), axis, backward)  2.58 us
  transfers between devices with their start and end apart: 5, of which 0 were waited for; matrix products, arithmetic and copies ran while one was open for 25% of the time, Pallas kernels for 53%

profile of v5, /device:TPU:1, one launch (start us, length us, event | category | flops | bytes accessed | tf_op | source)
XLA Modules:
  0.0 127.0 jit_solution(5512281396990937426)
XLA Ops:
  0.6 1.3 %collective-permute-start.4 = (bf16[2,1,30,512]{3,0,2,1:T(2,128)(2,1)}, bf16[2,1,30,512]{3,0,2,1:T(2,128)(2,1)S(1)}, u32[]{:S(2)}, u32[]{:S(2)}) collective-permute-start(bf16[2,1,30,512]{3,0,2,1:T(2,128)(2,1)} %bitcast.154), channel_id=1, source_target_pairs={{1,0},{2,1},{3,2},{4,3},{5,4},{6,5},{7,6},{8,7},{9,8},{10,9},{11,1... | collective-permute-start | bytes 184328 | tf_op jit(solution)/shard_map/ppermute | solution.py:38
  1.9 6.3 %collective-permute-start.3 = (bf16[2,1,30,512]{3,0,2,1:T(2,128)(2,1)}, bf16[2,1,30,512]{3,0,2,1:T(2,128)(2,1)S(1)}, u32[]{:S(2)}, u32[]{:S(2)}) collective-permute-start(bf16[2,1,30,512]{3,0,2,1:T(2,128)(2,1)} %bitcast.155), channel_id=1, source_target_pairs={{0,1},{1,2},{2,3},{3,4},{4,5},{5,6},{6,7},{7,8},{8,9},{9,10},{10,1... | collective-permute-start | bytes 184328 | tf_op jit(solution)/shard_map/ppermute | solution.py:35
  8.2 1.8 %fusion.36 = (bf16[2,1,60,256]{3,1,2,0:T(2,128)(2,1)}, bf16[2,1,60,256]{3,1,2,0:T(2,128)(2,1)S(1)}) fusion(bf16[2,2,60,256]{3,1,2,0:T(2,128)(2,1)} %bitcast.122), kind=kLoop, calls=%fused_computation.99 | loop fusion | bytes 245760 | tf_op jit(solution)/shard_map/slice | solution.py:36
  10.0 5.8 %collective-permute-start = (bf16[2,1,60,256]{3,1,2,0:T(2,128)(2,1)}, bf16[2,1,60,256]{3,1,2,0:T(2,128)(2,1)S(1)}, u32[]{:S(2)}, u32[]{:S(2)}) collective-permute-start(bf16[2,1,60,256]{3,1,2,0:T(2,128)(2,1)} %get-tuple-element.47), channel_id=1, source_target_pairs={{0,1},{1,2},{2,3},{3,4},{4,5},{5,6},{6,7},{7,8},{8,9},{9,10},{10,1... | collective-permute-start | bytes 184328 | tf_op jit(solution)/shard_map/ppermute | solution.py:35
  15.8 1.3 %collective-permute-start.1 = (bf16[2,1,60,256]{3,1,2,0:T(2,128)(2,1)S(1)}, bf16[2,1,60,256]{3,1,2,0:T(2,128)(2,1)S(1)}, u32[]{:S(2)}, u32[]{:S(2)}) collective-permute-start(bf16[2,1,60,256]{3,1,2,0:T(2,128)(2,1)S(1)} %get-tuple-element.48), channel_id=1, source_target_pairs={{1,0},{2,1},{3,2},{4,3},{5,4},{6,5},{7,6},{8,7},{9,8},{10,9},{11,1... | collective-permute-start | bytes 184328 | tf_op jit(solution)/shard_map/ppermute | solution.py:38
  17.1 0.9 copy.79
  18.0 1.0 concatenate.61
  19.1 0.7 reshape_squeeze.3.grad_ref
  19.8 0.1 copy.81
  19.9 0.0 collective-permute-done.3
  19.9 0.2 concatenate.60
  20.1 0.1 copy.80
  20.2 0.0 collective-permute-done.4
  20.2 0.2 concatenate.62
  20.4 0.1 copy.82
  20.5 0.2 maximum_bitcast_fusion.4
  20.7 0.0 copy-start.1
  20.7 1.2 reshape.328.lat_ref
  21.9 34.5 %shard_map.50 = (bf16[16,120,512]{2,1,0:T(8,128)(2,1)}, bf16[16,45,128]{2,1,0:T(8,128)(2,1)}) custom-call(bf16[120,512]{1,0:T(8,128)(2,1)} %reshape_squeeze.3.grad_ref, bf16[16,45,128]{2,1,0:T(8,128)(2,1)} %reshape.328.lat_ref), custom_call_target="tpu_custom_call" | custom-call | tf_op jit(solution)/shard_map/pallas_call | solution.py:188
  56.4 1.5 %reshape.329 = bf16[4,8,3,30,32]{4,3,2,1,0:T(8,128)(2,1)S(1)} reshape(bf16[16,45,128]{2,1,0:T(8,128)(2,1)} %get-tuple-element.5) | data formatting | bytes 368640 | tf_op jit(solution)/shard_map/reshape | solution.py:245
  57.9 0.7 copy.83
  58.6 1.0 fusion.34
  59.6 0.9 fusion.20
  60.5 0.0 collective-permute-done
  60.5 0.0 collective-permute-done.1
  60.5 0.0 copy-done.1
  60.5 1.1 pad_maximum_fusion.2
  61.6 1.5 %collective-permute-start.2 = (bf16[2,4,60,256]{3,1,2,0:T(4,128)(2,1)}, bf16[2,4,60,256]{3,1,2,0:T(4,128)(2,1)S(1)}, u32[]{:S(2)}, u32[]{:S(2)}) collective-permute-start(bf16[2,4,60,256]{3,1,2,0:T(4,128)(2,1)} %pad_maximum_fusion.2), channel_id=1, source_target_pairs={{16,0},{32,16},{48,32},{17,1},{33,17},{49,33},{18,2},{34,18},{50,3... | collective-permute-start | bytes 737288 | tf_op jit(solution)/shard_map/ppermute | solution.py:12
  63.1 0.0 copy-done.2
  63.1 2.2 %reshape.331 = f32[4,8,2,30,512]{4,3,2,1,0:T(8,128)} reshape(bf16[16,120,512]{2,1,0:T(8,128)(2,1)S(1)} %copy-done.2) | data formatting | bytes 5898240 | tf_op jit(solution)/shard_map/convert_element_type | solution.py:255
  65.4 2.8 %fusion.33 = (f32[4,8,2,29,256]{4,3,2,1,0:T(8,128)S(1)}, f32[4,8,2,29,256]{4,3,2,1,0:T(8,128)S(1)}) fusion(f32[4,8,2,30,512]{4,3,2,1,0:T(8,128)} %reshape.331), kind=kLoop, calls=%fused_computation.96 | loop fusion | bytes 7602176 | tf_op jit(solution)/shard_map/slice | solution.py:260
  68.1 0.0 copy-start.4
  68.2 0.0 copy-start.3
  68.2 0.0 copy-done.5
  68.2 0.9 fusion.29
  69.0 0.9 fusion.22
  70.0 1.0 fusion.24
  70.9 0.0 copy-done.4
  70.9 0.9 fusion.30
  71.8 0.9 fusion.26
  72.7 0.9 fusion.28
  73.6 0.0 copy-done.3
  73.6 0.9 fusion.31
  74.5 0.9 fusion.27
  75.3 0.0 copy-done
  75.3 1.4 %add_bitcast_fusion.2 = (f32[1,4,8,2,30,1,256]{6,4,3,2,1,5,0:T(8,128)S(1)}, f32[1,4,8,2,30,1,256]{6,4,3,2,1,5,0:T(8,128)S(1)}, f32[1,4,8,2,30,1,256]{6,4,3,2,1,5,0:T(8,128)S(1)}) fusion(f32[4,8,2,29,256]{4,3,2,1,0:T(8,128)S(1)} %get-tuple-element.17, f32[4,8,2,30,512]{4,3,2,1,0:T(8,128)S(1)} %copy-done, f32[4,8,2,29,256]{4,3,2,1,0:T(8,128)S(1)} %get-tuple-element.18), kind=kLoop, calls=%fused_computation.14 | loop fusion | flops 1474560 | bytes 13631488 | tf_op jit(solution)/shard_map/stack | solution.py:258
  76.7 1.5 %fusion.1 = (bf16[1,4,8,2,30,3,256]{6,4,3,2,1,5,0:T(8,128)(2,1)S(1)}, bf16[1,4,8,2,30,3,256]{6,4,3,2,1,5,0:T(8,128)(2,1)S(1)}) fusion(f32[1,4,8,2,30,1,256]{6,4,3,2,1,5,0:T(8,128)S(1)} %get-tuple-element.15, f32[1,4,8,2,30,1,256]{6,4,3,2,1,5,0:T(8,128)S(1)} %get-tuple-element.16, f32[1,4,8,2,30,1,256]{6,4,3,2,1,5,0:T(8,128)S(1)} %get-tuple-element.14), kind=kLoop, calls=%fused_computation.2 | loop fusion | flops 11796480 | bytes 11796480 | tf_op jit(solution)/shard_map/convert.1
  78.3 0.8 copy-done.6
  79.1 2.2 %fusion.9 = f32[32,9,3,2,256]{4,0,1,2,3:T(8,128)S(1)} fusion(bf16[9,4,8,2,30,32]{4,5,3,2,1,0:T(8,128)(2,1)S(1)} %copy-done.6, bf16[1,4,8,2,30,3,256]{6,4,3,2,1,5,0:T(8,128)(2,1)S(1)} %get-tuple-element.13, bf16[1,4,8,2,30,3,256]{6,4,3,2,1,5,0:T(8,128)(2,1)S(1)} %get-tuple-element.12), kind=kOutput, calls=%fused_computation.15 | convolution fusion | flops 1710489600 | bytes 8773632 | tf_op jit(solution)/shard_map/kbflsc,xbflsjo->ckjxo/dot_general | solution.py:269
  81.3 0.2 fusion.18
  81.4 0.6 copy.87
  82.0 1.4 %mul.31.term_ref = f32[16,108,128]{2,1,0:T(8,128)} reshape(f32[32,9,3,1,256]{4,2,1,0,3:T(4,128)S(1)} %copy.87) | data formatting | bytes 1769472 | tf_op jit(solution)/shard_map/mul | solution.py:272
  83.4 32.7 %shard_map.51 = f32[108,128]{1,0:T(8,128)} custom-call(f32[16,108,128]{2,1,0:T(8,128)} %mul.31.term_ref), custom_call_target="tpu_custom_call" | custom-call | tf_op jit(solution)/shard_map/pallas_call | solution.py:121
  116.1 0.8 reshape.330
  117.0 0.7 copy.89
  117.6 0.5 pad_maximum_fusion.3
  118.2 0.0 collective-permute-done.2
  118.2 0.5 pad_maximum_fusion.1
  118.7 0.2 pad_slice_fusion.23
  118.9 0.7 pad_slice_fusion.6
  119.6 0.7 pad_slice_fusion.7
  120.3 0.3 fusion.35
  121.3 5.0 %fusion.15 = bf16[2,30,512]{2,1,0:T(8,128)(2,1)S(1)} fusion(bf16[27,512,256,1,1,1]{2,1,0,5,4,3:T(8,128)(2,1)} %bitcast.156, bf16[2,1,2,30,2,27,256]{6,3,5,4,2,0,1:T(8,128)(2,1)S(1)} %copy_dynamic-update-slice_fusion), kind=kOutput, calls=%fused_computation.17 | convolution fusion | flops 1698785280 | bytes 10457088 | tf_op jit(solution)/shard_map/dot_general | solution.py:226
  126.3 0.7 copy.88
  (31 shorter events, 0.5 us)
Async XLA Ops:
  0.6 19.6 %collective-permute-start.4 = (bf16[2,1,30,512]{3,0,2,1:T(2,128)(2,1)}, bf16[2,1,30,512]{3,0,2,1:T(2,128)(2,1)S(1)}, u32[]{:S(2)}, u32[]{:S(2)}) collective-permute-start(bf16[2,1,30,512]{3,0,2,1:T(2,128)(2,1)} %bitcast.154), channel_id=1, source_target_pairs={{1,0},{2,1},{3,2},{4,3},{5,4},{6,5},{7,6},{8,7},{9,8},{10,9},{11,1... | collective-permute-start | bytes 184328 | tf_op jit(solution)/shard_map/ppermute | solution.py:38
  1.9 18.0 %collective-permute-start.3 = (bf16[2,1,30,512]{3,0,2,1:T(2,128)(2,1)}, bf16[2,1,30,512]{3,0,2,1:T(2,128)(2,1)S(1)}, u32[]{:S(2)}, u32[]{:S(2)}) collective-permute-start(bf16[2,1,30,512]{3,0,2,1:T(2,128)(2,1)} %bitcast.155), channel_id=1, source_target_pairs={{0,1},{1,2},{2,3},{3,4},{4,5},{5,6},{6,7},{7,8},{8,9},{9,10},{10,1... | collective-permute-start | bytes 184328 | tf_op jit(solution)/shard_map/ppermute | solution.py:35
  10.0 50.4 %collective-permute-start = (bf16[2,1,60,256]{3,1,2,0:T(2,128)(2,1)}, bf16[2,1,60,256]{3,1,2,0:T(2,128)(2,1)S(1)}, u32[]{:S(2)}, u32[]{:S(2)}) collective-permute-start(bf16[2,1,60,256]{3,1,2,0:T(2,128)(2,1)} %get-tuple-element.47), channel_id=1, source_target_pairs={{0,1},{1,2},{2,3},{3,4},{4,5},{5,6},{6,7},{7,8},{8,9},{9,10},{10,1... | collective-permute-start | bytes 184328 | tf_op jit(solution)/shard_map/ppermute | solution.py:35
  15.8 44.7 %collective-permute-start.1 = (bf16[2,1,60,256]{3,1,2,0:T(2,128)(2,1)S(1)}, bf16[2,1,60,256]{3,1,2,0:T(2,128)(2,1)S(1)}, u32[]{:S(2)}, u32[]{:S(2)}) collective-permute-start(bf16[2,1,60,256]{3,1,2,0:T(2,128)(2,1)S(1)} %get-tuple-element.48), channel_id=1, source_target_pairs={{1,0},{2,1},{3,2},{4,3},{5,4},{6,5},{7,6},{8,7},{9,8},{10,9},{11,1... | collective-permute-start | bytes 184328 | tf_op jit(solution)/shard_map/ppermute | solution.py:38
  20.7 39.8 %copy-start.1 = (bf16[1,2,2,60,256]{4,2,3,1,0:T(2,128)(2,1)S(1)}, bf16[1,2,2,60,256]{4,2,3,1,0:T(2,128)(2,1)}, u32[]{:S(2)}) copy-start(bf16[1,2,2,60,256]{4,2,3,1,0:T(2,128)(2,1)} %param.4) | copy-start | bytes 368644
  58.6 4.5 %copy-start.2 = (bf16[16,120,512]{2,1,0:T(8,128)(2,1)S(1)}, bf16[16,120,512]{2,1,0:T(8,128)(2,1)}, u32[]{:S(2)}) copy-start(bf16[16,120,512]{2,1,0:T(8,128)(2,1)} %get-tuple-element.4) | copy-start | bytes 5898244
  61.6 56.5 %collective-permute-start.2 = (bf16[2,4,60,256]{3,1,2,0:T(4,128)(2,1)}, bf16[2,4,60,256]{3,1,2,0:T(4,128)(2,1)S(1)}, u32[]{:S(2)}, u32[]{:S(2)}) collective-permute-start(bf16[2,4,60,256]{3,1,2,0:T(4,128)(2,1)} %pad_maximum_fusion.2), channel_id=1, source_target_pairs={{16,0},{32,16},{48,32},{17,1},{33,17},{49,33},{18,2},{34,18},{50,3... | collective-permute-start | bytes 737288 | tf_op jit(solution)/shard_map/ppermute | solution.py:12
  65.4 2.8 %copy-start.5 = (bf16[4,8,1,30,32]{3,4,2,1,0:T(8,128)(2,1)S(1)}, bf16[4,8,1,30,32]{3,4,2,1,0:T(8,128)(2,1)}, u32[]{:S(2)}) copy-start(bf16[4,8,1,30,32]{3,4,2,1,0:T(8,128)(2,1)} %get-tuple-element.20) | copy-start | bytes 184324
  68.1 2.8 %copy-start.4 = (bf16[4,8,1,30,32]{3,4,2,1,0:T(8,128)(2,1)S(1)}, bf16[4,8,1,30,32]{3,4,2,1,0:T(8,128)(2,1)}, u32[]{:S(2)}) copy-start(bf16[4,8,1,30,32]{3,4,2,1,0:T(8,128)(2,1)} %get-tuple-element.21) | copy-start | bytes 184324
  68.2 5.5 %copy-start.3 = (bf16[4,8,1,30,32]{3,4,2,1,0:T(8,128)(2,1)S(1)}, bf16[4,8,1,30,32]{3,4,2,1,0:T(8,128)(2,1)}, u32[]{:S(2)}) copy-start(bf16[4,8,1,30,32]{3,4,2,1,0:T(8,128)(2,1)} %get-tuple-element.19) | copy-start | bytes 184324
  69.0 6.3 %copy-start = (f32[4,8,2,30,512]{4,3,2,1,0:T(8,128)S(1)}, f32[4,8,2,30,512]{4,3,2,1,0:T(8,128)}, u32[]{:S(2)}) copy-start(f32[4,8,2,30,512]{4,3,2,1,0:T(8,128)} %reshape.331) | copy-start | bytes 11796484
  76.7 2.3 %copy-start.6 = (bf16[9,4,8,2,30,32]{4,5,3,2,1,0:T(8,128)(2,1)S(1)}, bf16[9,4,8,2,30,32]{4,5,3,2,1,0:T(8,128)(2,1)}, u32[]{:S(2)}) copy-start(bf16[9,4,8,2,30,32]{4,5,3,2,1,0:T(8,128)(2,1)} %fusion.27) | copy-start | bytes 3317764

commit v6 on v4

--- a/solution.py
+++ b/solution.py
@@ -144,9 +144,14 @@
     copies = []
     for d in range(1, count):
         target = (me + d) % count
-        for copy in (lat_copy(d, target, target, me), grad_copy(d, target, me)):
-            copy.start()
-            copies.append(copy)
+        copy = grad_copy(d, target, me)
+        copy.start()
+        copies.append(copy)
+    for d in range(1, count):
+        target = (me + d) % count
+        copy = lat_copy(d, target, target, me)
+        copy.start()
+        copies.append(copy)
     grad_buf[me] = grad_ref[...]
     lat_buf[me] = lat_ref[me]
     for d in range(1, count):

time: 129 us -> 128 us (level)
  no operation moved by 1% of the time
where the time goes in v6:
time: 128 us; the launch traced here: 126 us
  Pallas kernels  66.2 us (52%)
  local copies, waits for them, and re-layouts  27.3 us (21%)
  starting transfers between devices  16.1 us (13%)
  other arithmetic  8.03 us (6%)
  matrix products  7.23 us (6%)
    pallas_call x1, Pallas kernels, block_exchange(): pl.pallas_call(block_exchange_kernel, out_shape=(jax.ShapeDtypeStruct((co...  34.7 us
    pallas_call x1, Pallas kernels, scatter_sum(): pl.pallas_call(scatter_sum_kernel, out_shape=jax.ShapeDtypeStruct((rows,...  31.5 us
    ppermute x2, starting transfers between devices, with_halo(): lax.ppermute(lax.slice_in_dim(block, block.shape[dim] - width, None, axis...  12 us
    unnamed x48, local copies, waits for them, and re-layouts  8.15 us
    dot_general x1, matrix products, body(): lax.dot_general(patches, kernel.reshape(27, channels, outputs), (((1, 2),...  5.04 us
    slice x1, local copies, waits for them, and re-layouts, body(): left[:, :, :, 1:]  2.78 us
    unnamed x3, other arithmetic  2.62 us
    ppermute x2, starting transfers between devices, with_halo(): lax.ppermute(lax.slice_in_dim(block, 0, width, axis=dim), axis, backward)  2.58 us
  transfers between devices with their start and end apart: 5, of which 0 were waited for; matrix products, arithmetic and copies ran while one was open for 25% of the time, Pallas kernels for 53%

profile of v6, /device:TPU:1, one launch (start us, length us, event | category | flops | bytes accessed | tf_op | source)
XLA Modules:
  0.0 126.0 jit_solution(3572011695363320878)
XLA Ops:
  0.6 1.3 %collective-permute-start.4 = (bf16[2,1,30,512]{3,0,2,1:T(2,128)(2,1)}, bf16[2,1,30,512]{3,0,2,1:T(2,128)(2,1)S(1)}, u32[]{:S(2)}, u32[]{:S(2)}) collective-permute-start(bf16[2,1,30,512]{3,0,2,1:T(2,128)(2,1)} %bitcast.154), channel_id=1, source_target_pairs={{1,0},{2,1},{3,2},{4,3},{5,4},{6,5},{7,6},{8,7},{9,8},{10,9},{11,1... | collective-permute-start | bytes 184328 | tf_op jit(solution)/shard_map/ppermute | solution.py:38
  1.9 6.3 %collective-permute-start.3 = (bf16[2,1,30,512]{3,0,2,1:T(2,128)(2,1)}, bf16[2,1,30,512]{3,0,2,1:T(2,128)(2,1)S(1)}, u32[]{:S(2)}, u32[]{:S(2)}) collective-permute-start(bf16[2,1,30,512]{3,0,2,1:T(2,128)(2,1)} %bitcast.155), channel_id=1, source_target_pairs={{0,1},{1,2},{2,3},{3,4},{4,5},{5,6},{6,7},{7,8},{8,9},{9,10},{10,1... | collective-permute-start | bytes 184328 | tf_op jit(solution)/shard_map/ppermute | solution.py:35
  8.2 1.8 %fusion.36 = (bf16[2,1,60,256]{3,1,2,0:T(2,128)(2,1)}, bf16[2,1,60,256]{3,1,2,0:T(2,128)(2,1)S(1)}) fusion(bf16[2,2,60,256]{3,1,2,0:T(2,128)(2,1)} %bitcast.122), kind=kLoop, calls=%fused_computation.99 | loop fusion | bytes 245760 | tf_op jit(solution)/shard_map/slice | solution.py:36
  10.0 5.8 %collective-permute-start = (bf16[2,1,60,256]{3,1,2,0:T(2,128)(2,1)}, bf16[2,1,60,256]{3,1,2,0:T(2,128)(2,1)S(1)}, u32[]{:S(2)}, u32[]{:S(2)}) collective-permute-start(bf16[2,1,60,256]{3,1,2,0:T(2,128)(2,1)} %get-tuple-element.47), channel_id=1, source_target_pairs={{0,1},{1,2},{2,3},{3,4},{4,5},{5,6},{6,7},{7,8},{8,9},{9,10},{10,1... | collective-permute-start | bytes 184328 | tf_op jit(solution)/shard_map/ppermute | solution.py:35
  15.8 1.3 %collective-permute-start.1 = (bf16[2,1,60,256]{3,1,2,0:T(2,128)(2,1)S(1)}, bf16[2,1,60,256]{3,1,2,0:T(2,128)(2,1)S(1)}, u32[]{:S(2)}, u32[]{:S(2)}) collective-permute-start(bf16[2,1,60,256]{3,1,2,0:T(2,128)(2,1)S(1)} %get-tuple-element.48), channel_id=1, source_target_pairs={{1,0},{2,1},{3,2},{4,3},{5,4},{6,5},{7,6},{8,7},{9,8},{10,9},{11,1... | collective-permute-start | bytes 184328 | tf_op jit(solution)/shard_map/ppermute | solution.py:38
  17.1 0.9 copy.79
  18.0 1.0 concatenate.61
  19.1 0.7 reshape_squeeze.3.grad_ref
  19.8 0.1 copy.81
  19.9 0.0 collective-permute-done.3
  19.9 0.2 concatenate.60
  20.1 0.1 copy.80
  20.2 0.0 collective-permute-done.4
  20.2 0.2 concatenate.62
  20.4 0.1 copy.82
  20.5 0.2 maximum_bitcast_fusion.4
  20.7 0.0 copy-start.1
  20.7 1.2 reshape.328.lat_ref
  21.9 34.7 %shard_map.50 = (bf16[16,120,512]{2,1,0:T(8,128)(2,1)}, bf16[16,45,128]{2,1,0:T(8,128)(2,1)}) custom-call(bf16[120,512]{1,0:T(8,128)(2,1)} %reshape_squeeze.3.grad_ref, bf16[16,45,128]{2,1,0:T(8,128)(2,1)} %reshape.328.lat_ref), custom_call_target="tpu_custom_call" | custom-call | tf_op jit(solution)/shard_map/pallas_call | solution.py:167
  56.6 1.5 %reshape.329 = bf16[4,8,3,30,32]{4,3,2,1,0:T(8,128)(2,1)S(1)} reshape(bf16[16,45,128]{2,1,0:T(8,128)(2,1)} %get-tuple-element.5) | data formatting | bytes 368640 | tf_op jit(solution)/shard_map/reshape | solution.py:224
  58.1 0.7 copy.83
  58.8 1.0 fusion.34
  59.8 0.9 fusion.20
  60.7 0.0 collective-permute-done
  60.7 0.0 collective-permute-done.1
  60.7 0.0 copy-done.1
  60.7 1.1 pad_maximum_fusion.2
  61.8 1.5 %collective-permute-start.2 = (bf16[2,4,60,256]{3,1,2,0:T(4,128)(2,1)}, bf16[2,4,60,256]{3,1,2,0:T(4,128)(2,1)S(1)}, u32[]{:S(2)}, u32[]{:S(2)}) collective-permute-start(bf16[2,4,60,256]{3,1,2,0:T(4,128)(2,1)} %pad_maximum_fusion.2), channel_id=1, source_target_pairs={{16,0},{32,16},{48,32},{17,1},{33,17},{49,33},{18,2},{34,18},{50,3... | collective-permute-start | bytes 737288 | tf_op jit(solution)/shard_map/ppermute | solution.py:12
  63.3 0.0 copy-done.2
  63.3 2.2 %reshape.331 = f32[4,8,2,30,512]{4,3,2,1,0:T(8,128)} reshape(bf16[16,120,512]{2,1,0:T(8,128)(2,1)S(1)} %copy-done.2) | data formatting | bytes 5898240 | tf_op jit(solution)/shard_map/convert_element_type | solution.py:234
  65.5 2.8 %fusion.33 = (f32[4,8,2,29,256]{4,3,2,1,0:T(8,128)S(1)}, f32[4,8,2,29,256]{4,3,2,1,0:T(8,128)S(1)}) fusion(f32[4,8,2,30,512]{4,3,2,1,0:T(8,128)} %reshape.331), kind=kLoop, calls=%fused_computation.96 | loop fusion | bytes 7602176 | tf_op jit(solution)/shard_map/slice | solution.py:239
  68.3 0.0 copy-start.4
  68.3 0.0 copy-start.3
  68.4 0.0 copy-done.5
  68.4 0.9 fusion.29
  69.2 0.9 fusion.22
  70.2 1.0 fusion.24
  71.1 0.0 copy-done.4
  71.1 0.9 fusion.30
  72.0 0.9 fusion.26
  72.9 0.9 fusion.28
  73.8 0.0 copy-done.3
  73.8 0.9 fusion.31
  74.7 0.9 fusion.27
  75.5 0.0 copy-done
  75.5 1.4 %add_bitcast_fusion.2 = (f32[1,4,8,2,30,1,256]{6,4,3,2,1,5,0:T(8,128)S(1)}, f32[1,4,8,2,30,1,256]{6,4,3,2,1,5,0:T(8,128)S(1)}, f32[1,4,8,2,30,1,256]{6,4,3,2,1,5,0:T(8,128)S(1)}) fusion(f32[4,8,2,29,256]{4,3,2,1,0:T(8,128)S(1)} %get-tuple-element.17, f32[4,8,2,30,512]{4,3,2,1,0:T(8,128)S(1)} %copy-done, f32[4,8,2,29,256]{4,3,2,1,0:T(8,128)S(1)} %get-tuple-element.18), kind=kLoop, calls=%fused_computation.14 | loop fusion | flops 1474560 | bytes 13631488 | tf_op jit(solution)/shard_map/stack | solution.py:237
  76.9 1.5 %fusion.1 = (bf16[1,4,8,2,30,3,256]{6,4,3,2,1,5,0:T(8,128)(2,1)S(1)}, bf16[1,4,8,2,30,3,256]{6,4,3,2,1,5,0:T(8,128)(2,1)S(1)}) fusion(f32[1,4,8,2,30,1,256]{6,4,3,2,1,5,0:T(8,128)S(1)} %get-tuple-element.15, f32[1,4,8,2,30,1,256]{6,4,3,2,1,5,0:T(8,128)S(1)} %get-tuple-element.16, f32[1,4,8,2,30,1,256]{6,4,3,2,1,5,0:T(8,128)S(1)} %get-tuple-element.14), kind=kLoop, calls=%fused_computation.2 | loop fusion | flops 11796480 | bytes 11796480 | tf_op jit(solution)/shard_map/convert.1
  78.5 0.8 copy-done.6
  79.3 2.2 %fusion.9 = f32[32,9,3,2,256]{4,0,1,2,3:T(8,128)S(1)} fusion(bf16[9,4,8,2,30,32]{4,5,3,2,1,0:T(8,128)(2,1)S(1)} %copy-done.6, bf16[1,4,8,2,30,3,256]{6,4,3,2,1,5,0:T(8,128)(2,1)S(1)} %get-tuple-element.13, bf16[1,4,8,2,30,3,256]{6,4,3,2,1,5,0:T(8,128)(2,1)S(1)} %get-tuple-element.12), kind=kOutput, calls=%fused_computation.15 | convolution fusion | flops 1710489600 | bytes 8773632 | tf_op jit(solution)/shard_map/kbflsc,xbflsjo->ckjxo/dot_general | solution.py:248
  81.5 0.2 fusion.18
  81.6 0.6 copy.87
  82.2 1.4 %mul.31.term_ref = f32[16,108,128]{2,1,0:T(8,128)} reshape(f32[32,9,3,1,256]{4,2,1,0,3:T(4,128)S(1)} %copy.87) | data formatting | bytes 1769472 | tf_op jit(solution)/shard_map/mul | solution.py:251
  83.6 31.5 %shard_map.51 = f32[108,128]{1,0:T(8,128)} custom-call(f32[16,108,128]{2,1,0:T(8,128)} %mul.31.term_ref), custom_call_target="tpu_custom_call" | custom-call | tf_op jit(solution)/shard_map/pallas_call | solution.py:101
  115.2 0.8 reshape.330
  116.0 0.7 copy.89
  116.7 0.5 pad_maximum_fusion.3
  117.2 0.0 collective-permute-done.2
  117.2 0.5 pad_maximum_fusion.1
  117.8 0.2 pad_slice_fusion.23
  117.9 0.7 pad_slice_fusion.6
  118.6 0.7 pad_slice_fusion.7
  119.4 0.3 fusion.35
  120.3 5.0 %fusion.15 = bf16[2,30,512]{2,1,0:T(8,128)(2,1)S(1)} fusion(bf16[27,512,256,1,1,1]{2,1,0,5,4,3:T(8,128)(2,1)} %bitcast.156, bf16[2,1,2,30,2,27,256]{6,3,5,4,2,0,1:T(8,128)(2,1)S(1)} %copy_dynamic-update-slice_fusion), kind=kOutput, calls=%fused_computation.17 | convolution fusion | flops 1698785280 | bytes 10457088 | tf_op jit(solution)/shard_map/dot_general | solution.py:205
  125.4 0.7 copy.88
  (31 shorter events, 0.5 us)
Async XLA Ops:
  0.6 19.6 %collective-permute-start.4 = (bf16[2,1,30,512]{3,0,2,1:T(2,128)(2,1)}, bf16[2,1,30,512]{3,0,2,1:T(2,128)(2,1)S(1)}, u32[]{:S(2)}, u32[]{:S(2)}) collective-permute-start(bf16[2,1,30,512]{3,0,2,1:T(2,128)(2,1)} %bitcast.154), channel_id=1, source_target_pairs={{1,0},{2,1},{3,2},{4,3},{5,4},{6,5},{7,6},{8,7},{9,8},{10,9},{11,1... | collective-permute-start | bytes 184328 | tf_op jit(solution)/shard_map/ppermute | solution.py:38
  1.9 18.0 %collective-permute-start.3 = (bf16[2,1,30,512]{3,0,2,1:T(2,128)(2,1)}, bf16[2,1,30,512]{3,0,2,1:T(2,128)(2,1)S(1)}, u32[]{:S(2)}, u32[]{:S(2)}) collective-permute-start(bf16[2,1,30,512]{3,0,2,1:T(2,128)(2,1)} %bitcast.155), channel_id=1, source_target_pairs={{0,1},{1,2},{2,3},{3,4},{4,5},{5,6},{6,7},{7,8},{8,9},{9,10},{10,1... | collective-permute-start | bytes 184328 | tf_op jit(solution)/shard_map/ppermute | solution.py:35
  10.0 50.6 %collective-permute-start = (bf16[2,1,60,256]{3,1,2,0:T(2,128)(2,1)}, bf16[2,1,60,256]{3,1,2,0:T(2,128)(2,1)S(1)}, u32[]{:S(2)}, u32[]{:S(2)}) collective-permute-start(bf16[2,1,60,256]{3,1,2,0:T(2,128)(2,1)} %get-tuple-element.47), channel_id=1, source_target_pairs={{0,1},{1,2},{2,3},{3,4},{4,5},{5,6},{6,7},{7,8},{8,9},{9,10},{10,1... | collective-permute-start | bytes 184328 | tf_op jit(solution)/shard_map/ppermute | solution.py:35
  15.8 44.9 %collective-permute-start.1 = (bf16[2,1,60,256]{3,1,2,0:T(2,128)(2,1)S(1)}, bf16[2,1,60,256]{3,1,2,0:T(2,128)(2,1)S(1)}, u32[]{:S(2)}, u32[]{:S(2)}) collective-permute-start(bf16[2,1,60,256]{3,1,2,0:T(2,128)(2,1)S(1)} %get-tuple-element.48), channel_id=1, source_target_pairs={{1,0},{2,1},{3,2},{4,3},{5,4},{6,5},{7,6},{8,7},{9,8},{10,9},{11,1... | collective-permute-start | bytes 184328 | tf_op jit(solution)/shard_map/ppermute | solution.py:38
  20.7 40.0 %copy-start.1 = (bf16[1,2,2,60,256]{4,2,3,1,0:T(2,128)(2,1)S(1)}, bf16[1,2,2,60,256]{4,2,3,1,0:T(2,128)(2,1)}, u32[]{:S(2)}) copy-start(bf16[1,2,2,60,256]{4,2,3,1,0:T(2,128)(2,1)} %param.4) | copy-start | bytes 368644
  58.8 4.5 %copy-start.2 = (bf16[16,120,512]{2,1,0:T(8,128)(2,1)S(1)}, bf16[16,120,512]{2,1,0:T(8,128)(2,1)}, u32[]{:S(2)}) copy-start(bf16[16,120,512]{2,1,0:T(8,128)(2,1)} %get-tuple-element.4) | copy-start | bytes 5898244
  61.8 55.4 %collective-permute-start.2 = (bf16[2,4,60,256]{3,1,2,0:T(4,128)(2,1)}, bf16[2,4,60,256]{3,1,2,0:T(4,128)(2,1)S(1)}, u32[]{:S(2)}, u32[]{:S(2)}) collective-permute-start(bf16[2,4,60,256]{3,1,2,0:T(4,128)(2,1)} %pad_maximum_fusion.2), channel_id=1, source_target_pairs={{16,0},{32,16},{48,32},{17,1},{33,17},{49,33},{18,2},{34,18},{50,3... | collective-permute-start | bytes 737288 | tf_op jit(solution)/shard_map/ppermute | solution.py:12
  65.5 2.8 %copy-start.5 = (bf16[4,8,1,30,32]{3,4,2,1,0:T(8,128)(2,1)S(1)}, bf16[4,8,1,30,32]{3,4,2,1,0:T(8,128)(2,1)}, u32[]{:S(2)}) copy-start(bf16[4,8,1,30,32]{3,4,2,1,0:T(8,128)(2,1)} %get-tuple-element.20) | copy-start | bytes 184324
  68.3 2.8 %copy-start.4 = (bf16[4,8,1,30,32]{3,4,2,1,0:T(8,128)(2,1)S(1)}, bf16[4,8,1,30,32]{3,4,2,1,0:T(8,128)(2,1)}, u32[]{:S(2)}) copy-start(bf16[4,8,1,30,32]{3,4,2,1,0:T(8,128)(2,1)} %get-tuple-element.21) | copy-start | bytes 184324
  68.3 5.5 %copy-start.3 = (bf16[4,8,1,30,32]{3,4,2,1,0:T(8,128)(2,1)S(1)}, bf16[4,8,1,30,32]{3,4,2,1,0:T(8,128)(2,1)}, u32[]{:S(2)}) copy-start(bf16[4,8,1,30,32]{3,4,2,1,0:T(8,128)(2,1)} %get-tuple-element.19) | copy-start | bytes 184324
  69.2 6.3 %copy-start = (f32[4,8,2,30,512]{4,3,2,1,0:T(8,128)S(1)}, f32[4,8,2,30,512]{4,3,2,1,0:T(8,128)}, u32[]{:S(2)}) copy-start(f32[4,8,2,30,512]{4,3,2,1,0:T(8,128)} %reshape.331) | copy-start | bytes 11796484
  76.9 2.3 %copy-start.6 = (bf16[9,4,8,2,30,32]{4,5,3,2,1,0:T(8,128)(2,1)S(1)}, bf16[9,4,8,2,30,32]{4,5,3,2,1,0:T(8,128)(2,1)}, u32[]{:S(2)}) copy-start(bf16[9,4,8,2,30,32]{4,5,3,2,1,0:T(8,128)(2,1)} %fusion.27) | copy-start | bytes 3317764
